TPU v7x, 1024 devices: a whole 4x4x32 slice. The times are simulated.
1024 devices in a mesh: section: 128 (over z, y_hi, core), dp: 8 (over y_lo, x).
Axes of the slice: x: 4, y: 4 (y_hi: 2, y_lo: 2; y = y_hi * 2 + y_lo), z: 32, core: 2. Of those that a mesh axis runs over, the one named last changes fastest.
Arguments:
- w_up: bfloat16 [128, 32, 128, 128], P('section'), may hold values from -0.375 to 0.375
- up_index: int32 [128, 32], P('section'), may hold values from 0 to 31
- w_down: bfloat16 [128, 32, 128, 128], P('section'), may hold values from -0.375 to 0.375
- down_index: int32 [128, 32], P('section'), may hold values from 0 to 31
- tick_order: int32 [128, 2], P('section'), may hold values from 0 to 1, each once within a row
- values_in: bfloat16 [128, 64, 4096], P('section', 'dp'), may hold values from -6 to 6
- score_grad_in: bfloat16 [128, 64, 4096], P('section', 'dp'), may hold values from -6 to 6
- tangent_in: bfloat16 [128, 64, 4096], P('section', 'dp'), may hold values from -6 to 6
- state_adjoint_in: bfloat16 [128, 64, 4096], P('section', 'dp'), may hold values from -6 to 6
- saved_back: bfloat16 [128, 2, 64, 4096], P('section', None, 'dp'), may hold values from -6 to 6
- saved_tan: bfloat16 [128, 2, 64, 4096], P('section', None, 'dp'), may hold values from -6 to 6
- saved_second: bfloat16 [128, 2, 64, 4096], P('section', None, 'dp'), may hold values from -6 to 6
- saved_second_tan: bfloat16 [128, 2, 64, 4096], P('section', None, 'dp'), may hold values from -6 to 6
- saved_second_grad: bfloat16 [128, 2, 64, 4096], P('section', None, 'dp'), may hold values from -6 to 6
Outputs:
- values_out: bfloat16 [128, 64, 4096], P('section', 'dp')
- score_grad_out: bfloat16 [128, 64, 4096], P('section', 'dp')
- tangent_out: bfloat16 [128, 64, 4096], P('section', 'dp')
- state_adjoint_out: bfloat16 [128, 64, 4096], P('section', 'dp')
- grad_up: bfloat16 [128, 32, 128, 128], P('section', 'dp')
- grad_down: bfloat16 [128, 32, 128, 128], P('section', 'dp')
Inputs may be any that keep to these rules, and one draw needn't show every extreme that they name: up_index[s, j] is the input block that hidden block j of layer s reads. down_index[s, i] is the hidden block that output block i of layer s reads. `tick_order`: each row is a permutation of the 2 slots.
All inputs are finite; a program needn't handle non-finite values.
Results may differ from a plain program's by a relative error of at most 0.023.
Values may be sent and summed in bfloat16 or wider, within the bound.
A program may use at most 32 MiB of HBM per device.

v0:
```python
import jax
import jax.numpy as jnp
from jax import lax
from jax.sharding import PartitionSpec as P

BLOCK = 128


def from_behind(block, axis, distance):
    devices = range(lax.axis_size(axis))
    route = [((i - distance) % len(devices), i) for i in devices]
    return lax.ppermute(block, axis, route)


def silu_parts(inputs):
    logistic = jax.nn.sigmoid(inputs)
    slopes = logistic * (1.0 + inputs * (1.0 - logistic))
    curves = logistic * (1.0 - logistic) * (2.0 + inputs * (1.0 - 2.0 * logistic))
    return (inputs * logistic, slopes, curves)


def block_map(matrix, weight, block_table):
    block_width = weight.shape[-1]
    row_count = matrix.shape[0]
    pieces = matrix.reshape(row_count, -1, block_width)
    picked = jnp.take(pieces, block_table, axis=1)
    result = jnp.einsum("rnk,nkj->rnj", picked, weight, preferred_element_type=jnp.float32)
    return result.reshape(row_count, -1)


def block_map_back(matrix, weight, block_table, block_count):
    block_width = weight.shape[-1]
    row_count = matrix.shape[0]
    pieces = matrix.reshape(row_count, -1, block_width)
    partial_value = jnp.einsum("rnj,nkj->rnk", pieces, weight, preferred_element_type=jnp.float32)
    placing = (block_table[:, None] == jnp.arange(block_count, dtype=jnp.int32)[None, :]).astype(
        jnp.bfloat16
    )
    high_part = partial_value.astype(jnp.bfloat16)
    low_part = (partial_value - high_part.astype(jnp.float32)).astype(jnp.bfloat16)
    result = jnp.einsum("rnk,nc->rck", high_part, placing, preferred_element_type=jnp.float32)
    result = result + jnp.einsum(
        "rnk,nc->rck", low_part, placing, preferred_element_type=jnp.float32
    )
    return result.reshape(row_count, -1)


def grad_blocks(inputs, cotangents, block_table):
    row_count = inputs.shape[0]
    pieces = inputs.reshape(row_count, -1, BLOCK)
    picked = jnp.take(pieces, block_table, axis=1)
    cot_part = cotangents.reshape(row_count, -1, BLOCK)
    return jnp.einsum("rnk,rnj->nkj", picked, cot_part, preferred_element_type=jnp.float32)


def on_device(
    w_up,
    up_index,
    w_down,
    down_index,
    tick_order,
    values_in,
    score_grad_in,
    tangent_in,
    state_adjoint_in,
    saved_back,
    saved_tan,
    saved_second,
    saved_second_tan,
    saved_second_grad,
):
    up_weight = w_up[0]
    up_table = up_index[0]
    down_weight = w_down[0]
    down_table = down_index[0]
    hidden_blocks = up_weight.shape[0]
    model_blocks = down_weight.shape[0]
    row_count = values_in.shape[1]
    replicas = lax.axis_size("dp")
    row_scale = 1.0 / (row_count * replicas)
    values = values_in[0]
    score_grad = score_grad_in[0]
    tangent = tangent_in[0]
    adjoint = state_adjoint_in[0]
    up_inputs = []
    up_cotangents = []
    down_inputs = []
    down_cotangents = []
    for tick_number in range(tick_order.shape[1]):
        slot_index = tick_order[0, tick_number]
        back_input = lax.dynamic_index_in_dim(saved_back[0], slot_index, 0, keepdims=False)
        tangent_input = lax.dynamic_index_in_dim(saved_tan[0], slot_index, 0, keepdims=False)
        second_input = lax.dynamic_index_in_dim(saved_second[0], slot_index, 0, keepdims=False)
        second_tangent = lax.dynamic_index_in_dim(
            saved_second_tan[0], slot_index, 0, keepdims=False
        )
        second_grad = lax.dynamic_index_in_dim(saved_second_grad[0], slot_index, 0, keepdims=False)
        raised = block_map(
            jnp.concatenate(
                [values, tangent_input, tangent, back_input, second_input, second_tangent], 0
            ),
            up_weight,
            up_table,
        )
        (
            raised_values,
            raised_tangent_input,
            raised_tangent,
            raised_back,
            raised_second,
            raised_second_tangent,
        ) = jnp.split(raised, 6, 0)
        hidden_values = silu_parts(raised_values)[0].astype(jnp.bfloat16)
        tangent_hidden = (silu_parts(raised_tangent_input)[1] * raised_tangent).astype(jnp.bfloat16)
        lowered = block_map(
            jnp.concatenate([hidden_values, tangent_hidden], 0), down_weight, down_table
        )
        lowered_values, lowered_tangent = jnp.split(lowered, 2, 0)
        new_values = (values.astype(jnp.float32) + lowered_values).astype(jnp.bfloat16)
        new_tangent = (tangent.astype(jnp.float32) + lowered_tangent).astype(jnp.bfloat16)
        active_back, slope_back, unused_curve = silu_parts(raised_back)
        active_second, slope_second, curve_second = silu_parts(raised_second)
        pulled = block_map_back(
            jnp.concatenate([score_grad, second_grad, adjoint], 0),
            down_weight,
            down_table,
            hidden_blocks,
        )
        pulled_score, pulled_second, pulled_adjoint = jnp.split(pulled, 3, 0)
        gate_back = (slope_back * pulled_score).astype(jnp.bfloat16)
        second_push = (
            slope_second * pulled_adjoint + curve_second * pulled_second * raised_second_tangent
        ).astype(jnp.bfloat16)
        returned = block_map_back(
            jnp.concatenate([gate_back, second_push], 0), up_weight, up_table, model_blocks
        )
        returned_score, returned_adjoint = jnp.split(returned, 2, 0)
        new_score_grad = (score_grad.astype(jnp.float32) + returned_score).astype(jnp.bfloat16)
        new_adjoint = (adjoint.astype(jnp.float32) + returned_adjoint).astype(jnp.bfloat16)
        hidden_back = active_back.astype(jnp.bfloat16)
        hidden_second = active_second.astype(jnp.bfloat16)
        tangent_second = (slope_second * raised_second_tangent).astype(jnp.bfloat16)
        gated_second = (slope_second * pulled_second).astype(jnp.bfloat16)
        up_inputs += [back_input, second_input, second_tangent]
        up_cotangents += [gate_back, second_push, gated_second]
        down_inputs += [hidden_back, hidden_second, tangent_second]
        down_cotangents += [score_grad, adjoint, second_grad]
        values, tangent = from_behind((new_values, new_tangent), "section", 1)
        score_grad, adjoint = from_behind((new_score_grad, new_adjoint), "section", -1)
    up_rows = jnp.concatenate(up_inputs, 0)
    up_cot_rows = jnp.concatenate(up_cotangents, 0)
    down_rows = jnp.concatenate(down_inputs, 0)
    down_cot_rows = jnp.concatenate(down_cotangents, 0)
    up_term = grad_blocks(up_rows, up_cot_rows, up_table) * row_scale
    down_term = grad_blocks(down_rows, down_cot_rows, down_table) * row_scale
    grad_up, grad_down = (
        lax.psum_scatter(
            up_term.astype(jnp.bfloat16), "dp", scatter_dimension=0, tiled=True
        ).astype(jnp.float32),
        lax.psum_scatter(
            down_term.astype(jnp.bfloat16), "dp", scatter_dimension=0, tiled=True
        ).astype(jnp.float32),
    )
    grad_up = grad_up.astype(jnp.bfloat16)
    grad_down = grad_down.astype(jnp.bfloat16)
    return (
        values[None],
        score_grad[None],
        tangent[None],
        adjoint[None],
        grad_up[None],
        grad_down[None],
    )


def solution(mesh):
    placed = (
        P("section", None, None, None),
        P("section", None),
        P("section", None, None, None),
        P("section", None),
        P("section", None),
        P("section", "dp", None),
        P("section", "dp", None),
        P("section", "dp", None),
        P("section", "dp", None),
        P("section", None, "dp", None),
        P("section", None, "dp", None),
        P("section", None, "dp", None),
        P("section", None, "dp", None),
        P("section", None, "dp", None),
    )
    return jax.shard_map(
        on_device,
        mesh=mesh,
        in_specs=placed,
        out_specs=(
            P("section", "dp", None),
            P("section", "dp", None),
            P("section", "dp", None),
            P("section", "dp", None),
            P("section", "dp", None, None),
            P("section", "dp", None, None),
        ),
        check_vma=False,
    )
```

profile of v0, /device:TPU:6, one launch (start us, length us, event | category | flops | bytes accessed | tf_op | source)
XLA Modules:
  0.0 190.3 jit_solution(10221817564089754241)
XLA Ops:
  7.2 0.8 compare_select_fusion
  8.0 0.7 compare_and_fusion
  8.7 1.3 fusion.128
  11.3 0.9 constant_dynamic-update-slice_fusion.35
  12.2 0.9 constant_dynamic-update-slice_fusion.5
  13.7 0.9 constant_dynamic-update-slice_fusion.34
  14.6 1.5 constant_dynamic-update-slice_fusion.33
  16.1 0.9 constant_dynamic-update-slice_fusion.3
  17.0 0.9 constant_dynamic-update-slice_fusion.17
  20.8 0.7 fusion.72
  21.5 2.0 %collective-permute-start = (bf16[8,4096]{1,0:T(8,128)(2,1)}, bf16[8,4096]{1,0:T(8,128)(2,1)S(1)}, u32[]{:S(2)}, u32[]{:S(2)}) collective-permute-start(bf16[8,4096]{1,0:T(8,128)(2,1)} %get-tuple-element.45), channel_id=1, source_target_pairs={{1016,0},{0,8},{8,16},{16,24},{24,32},{32,40},{40,48},{48,56},{56,... | collective-permute-start | bytes 196616 | tf_op jit(solution)/shard_map/ppermute | solution.py:12
  23.6 5.2 %collective-permute-start.1 = (bf16[8,4096]{1,0:T(8,128)(2,1)}, bf16[8,4096]{1,0:T(8,128)(2,1)S(1)}, u32[]{:S(2)}, u32[]{:S(2)}) collective-permute-start(bf16[8,4096]{1,0:T(8,128)(2,1)} %get-tuple-element.44), channel_id=1, source_target_pairs={{1016,0},{0,8},{8,16},{16,24},{24,32},{32,40},{40,48},{48,56},{56,... | collective-permute-start | bytes 196616 | tf_op jit(solution)/shard_map/ppermute | solution.py:12
  28.9 0.7 subtract_convert_fusion.1
  30.6 0.6 subtract_convert_fusion.3
  31.7 0.7 fusion.63
  32.4 17.4 %collective-permute-start.3 = (bf16[8,4096]{1,0:T(8,128)(2,1)}, bf16[8,4096]{1,0:T(8,128)(2,1)S(1)}, u32[]{:S(2)}, u32[]{:S(2)}) collective-permute-start(bf16[8,4096]{1,0:T(8,128)(2,1)} %fusion.63), channel_id=1, source_target_pairs={{8,0},{16,8},{24,16},{32,24},{40,32},{48,40},{56,48},{64,56},{72,6... | collective-permute-start | bytes 196616 | tf_op jit(solution)/shard_map/ppermute | solution.py:12
  49.8 0.7 fusion.62
  50.6 2.6 %collective-permute-start.4 = (bf16[8,4096]{1,0:T(8,128)(2,1)}, bf16[8,4096]{1,0:T(8,128)(2,1)S(1)}, u32[]{:S(2)}, u32[]{:S(2)}) collective-permute-start(bf16[8,4096]{1,0:T(8,128)(2,1)} %fusion.62), channel_id=1, source_target_pairs={{8,0},{16,8},{24,16},{32,24},{40,32},{48,40},{56,48},{64,56},{72,6... | collective-permute-start | bytes 196616 | tf_op jit(solution)/shard_map/ppermute | solution.py:12
  53.2 0.8 copy-done.4
  54.0 0.7 copy-done.6
  56.5 0.9 constant_dynamic-update-slice_fusion.10
  57.4 0.9 constant_dynamic-update-slice_fusion.14
  58.3 0.9 constant_dynamic-update-slice_fusion.13
  59.2 0.9 constant_dynamic-update-slice_fusion.12
  60.1 0.8 copy-done.8
  60.9 0.7 gather_fusion.2
  62.1 0.6 constant_dynamic-update-slice_fusion.32
  64.1 0.7 subtract_convert_fusion
  65.1 0.7 constant_dynamic-update-slice_fusion.26
  66.3 0.8 constant_dynamic-update-slice_fusion.20
  67.0 0.7 constant_dynamic-update-slice_fusion.19
  67.8 0.8 constant_dynamic-update-slice_fusion.24
  68.5 1.7 gather_fusion.5
  70.3 2.6 %multiply_convert_fusion = bf16[32,128,128]{2,1,0:T(8,128)(2,1)} fusion(bf16[48,32,128]{2,0,1:T(8,128)(2,1)} %get-tuple-element.8, bf16[32,48,128]{2,1,0:T(8,128)(2,1)S(1)} %gather_fusion.5, pred[32]{0:T(512)(128)(4,1)S(1)} %get-tuple-element.62), kind=kOutput, calls=%fused_computation.6 | convolution fusion | flops 51576832 | bytes 1835040 | tf_op jit(solution)/shard_map/rnk,rnj->nkj/dot_general | solution.py:53
  72.9 1.7 gather_fusion.4
  74.7 0.6 subtract_convert_fusion.2
  75.7 0.7 fusion.60
  76.4 5.1 %collective-permute-start.7 = (bf16[8,4096]{1,0:T(8,128)(2,1)}, bf16[8,4096]{1,0:T(8,128)(2,1)}, u32[]{:S(2)}, u32[]{:S(2)}) collective-permute-start(bf16[8,4096]{1,0:T(8,128)(2,1)} %fusion.60), channel_id=1, source_target_pairs={{8,0},{16,8},{24,16},{32,24},{40,32},{48,40},{56,48},{64,56},{72,6... | collective-permute-start | bytes 196616 | tf_op jit(solution)/shard_map/ppermute | solution.py:12
  81.6 1.5 multiply_convert_fusion.1
  83.2 2.4 %collective-permute-start.5 = (bf16[8,4096]{1,0:T(8,128)(2,1)S(1)}, bf16[8,4096]{1,0:T(8,128)(2,1)S(1)}, u32[]{:S(2)}, u32[]{:S(2)}) collective-permute-start(bf16[8,4096]{1,0:T(8,128)(2,1)S(1)} %fusion.61), channel_id=1, source_target_pairs={{8,0},{16,8},{24,16},{32,24},{40,32},{48,40},{56,48},{64,56},{72,6... | collective-permute-start | bytes 196616 | tf_op jit(solution)/shard_map/ppermute | solution.py:12
  85.8 0.8 gather_fusion.3
  87.1 1.9 %collective-permute-start.2 = (bf16[8,4096]{1,0:T(8,128)(2,1)S(1)}, bf16[8,4096]{1,0:T(8,128)(2,1)S(1)}, u32[]{:S(2)}, u32[]{:S(2)}) collective-permute-start(bf16[8,4096]{1,0:T(8,128)(2,1)S(1)} %get-tuple-element.41), channel_id=1, source_target_pairs={{1016,0},{0,8},{8,16},{16,24},{24,32},{32,40},{40,48},{48,56},{56,... | collective-permute-start | bytes 196616 | tf_op jit(solution)/shard_map/ppermute | solution.py:12
  89.1 1.9 %collective-permute-start.6 = (bf16[8,4096]{1,0:T(8,128)(2,1)S(1)}, bf16[8,4096]{1,0:T(8,128)(2,1)S(1)}, u32[]{:S(2)}, u32[]{:S(2)}) collective-permute-start(bf16[8,4096]{1,0:T(8,128)(2,1)S(1)} %get-tuple-element.40), channel_id=1, source_target_pairs={{1016,0},{0,8},{8,16},{16,24},{24,32},{32,40},{40,48},{48,56},{56,... | collective-permute-start | bytes 196616 | tf_op jit(solution)/shard_map/ppermute | solution.py:12
  91.0 6.0 %collective-permute-done.2 = bf16[8,4096]{1,0:T(8,128)(2,1)S(1)} collective-permute-done((bf16[8,4096]{1,0:T(8,128)(2,1)S(1)}, bf16[8,4096]{1,0:T(8,128)(2,1)S(1)}, u32[]{:S(2)}, u32[]{:S(2)}) %collective-permute-start.2) | collective-permute-done | bytes 65568 | tf_op jit(solution)/shard_map/ppermute | solution.py:12
  97.0 1.2 collective-permute-done.6
  98.3 21.7 %reduce-scatter.5.cloned.1.call-done = bf16[4,128,128]{2,1,0:T(8,128)(2,1)} async-done(((bf16[32,128,128]{2,1,0:T(8,128)(2,1)}), bf16[4,128,128]{2,1,0:T(8,128)(2,1)}) %reduce-scatter.5.cloned.1.call-update) | async-done | bytes 131088 | tf_op jit(solution)/shard_map/reduce_scatter | solution.py:160
  120.0 60.1 %reduce-scatter.3.cloned.1.call-done = bf16[4,128,128]{2,1,0:T(8,128)(2,1)} async-done(((bf16[32,128,128]{2,1,0:T(8,128)(2,1)}), bf16[4,128,128]{2,1,0:T(8,128)(2,1)}) %reduce-scatter.3.cloned.1.call-update) | async-done | bytes 131088 | tf_op jit(solution)/shard_map/reduce_scatter | solution.py:157
  181.9 1.5 copy.101
  (92 shorter events, 10.1 us)
Async XLA Ops:
  7.2 11.5 %copy-start = (bf16[1,32,128,128]{3,2,1,0:T(8,128)(2,1)S(1)}, bf16[1,32,128,128]{3,2,1,0:T(8,128)(2,1)}, u32[]{:S(2)}) copy-start(bf16[1,32,128,128]{3,2,1,0:T(8,128)(2,1)} %param.18) | copy-start | bytes 3145732
  7.2 10.7 %copy-start.16 = (bf16[1,2,8,4096]{3,2,1,0:T(8,128)(2,1)S(1)}, bf16[1,2,8,4096]{3,2,1,0:T(8,128)(2,1)}, u32[]{:S(2)}) copy-start(bf16[1,2,8,4096]{3,2,1,0:T(8,128)(2,1)} %param.29) | copy-start | bytes 393220
  7.2 10.7 %copy-start.17 = (bf16[1,2,8,4096]{3,2,1,0:T(8,128)(2,1)S(1)}, bf16[1,2,8,4096]{3,2,1,0:T(8,128)(2,1)}, u32[]{:S(2)}) copy-start(bf16[1,2,8,4096]{3,2,1,0:T(8,128)(2,1)} %param.30) | copy-start | bytes 393220
  7.2 112.8 %reduce-scatter.5.cloned.1.call-start = ((), (), s32[]{:S(2)}) async-start(), calls=%async_computation.3 | async-start | bytes 1179648 | tf_op jit(solution)/shard_map/reduce_scatter | solution.py:160
  13.0 6.1 %copy-start.22 = (s32[1024]{0:T(1024)}, s32[1024]{0:T(1024)S(1)}, u32[]{:S(2)}) copy-start(s32[1024]{0:T(1024)S(1)} %pad_clamp_fusion.1) | copy-start | bytes 12292
  16.1 1.9 copy-start.5
  19.1 1.2 copy-start.1
  19.3 2.3 %copy-start.21 = (s32[1024]{0:T(1024)}, s32[1024]{0:T(1024)S(1)}, u32[]{:S(2)}) copy-start(s32[1024]{0:T(1024)S(1)} %pad_clamp_fusion) | copy-start | bytes 12292
  19.9 0.9 copy-start.10
  19.9 0.9 copy-start.11
  20.4 8.5 %copy-start.2 = (bf16[1,8,4096]{2,1,0:T(8,128)(2,1)S(1)}, bf16[1,8,4096]{2,1,0:T(8,128)(2,1)}, u32[]{:S(2)}) copy-start(bf16[1,8,4096]{2,1,0:T(8,128)(2,1)} %param.24) | copy-start | bytes 196612
  20.4 8.5 %copy-start.3 = (bf16[1,8,4096]{2,1,0:T(8,128)(2,1)S(1)}, bf16[1,8,4096]{2,1,0:T(8,128)(2,1)}, u32[]{:S(2)}) copy-start(bf16[1,8,4096]{2,1,0:T(8,128)(2,1)} %param.26) | copy-start | bytes 196612
  20.4 8.5 %copy-start.9 = (bf16[8,32,128]{2,0,1:T(8,128)(2,1)S(1)}, bf16[8,32,128]{2,0,1:T(8,128)(2,1)}, u32[]{:S(2)}) copy-start(bf16[8,32,128]{2,0,1:T(8,128)(2,1)} %get-tuple-element.11) | copy-start | bytes 196612
  21.5 8.0 %copy-start.20 = (s32[1,32]{1,0:T(1,128)S(1)}, s32[1,32]{1,0:T(1,128)}, u32[]{:S(2)}) copy-start(s32[1,32]{1,0:T(1,128)} %param.21) | copy-start | bytes 388
  21.5 34.9 %collective-permute-start = (bf16[8,4096]{1,0:T(8,128)(2,1)}, bf16[8,4096]{1,0:T(8,128)(2,1)S(1)}, u32[]{:S(2)}, u32[]{:S(2)}) collective-permute-start(bf16[8,4096]{1,0:T(8,128)(2,1)} %get-tuple-element.45), channel_id=1, source_target_pairs={{1016,0},{0,8},{8,16},{16,24},{24,32},{32,40},{40,48},{48,56},{56,... | collective-permute-start | bytes 196616 | tf_op jit(solution)/shard_map/ppermute | solution.py:12
  23.6 33.8 %collective-permute-start.1 = (bf16[8,4096]{1,0:T(8,128)(2,1)}, bf16[8,4096]{1,0:T(8,128)(2,1)S(1)}, u32[]{:S(2)}, u32[]{:S(2)}) collective-permute-start(bf16[8,4096]{1,0:T(8,128)(2,1)} %get-tuple-element.44), channel_id=1, source_target_pairs={{1016,0},{0,8},{8,16},{16,24},{24,32},{32,40},{40,48},{48,56},{56,... | collective-permute-start | bytes 196616 | tf_op jit(solution)/shard_map/ppermute | solution.py:12
  30.5 0.8 copy-start.19
  32.4 29.8 %collective-permute-start.3 = (bf16[8,4096]{1,0:T(8,128)(2,1)}, bf16[8,4096]{1,0:T(8,128)(2,1)S(1)}, u32[]{:S(2)}, u32[]{:S(2)}) collective-permute-start(bf16[8,4096]{1,0:T(8,128)(2,1)} %fusion.63), channel_id=1, source_target_pairs={{8,0},{16,8},{24,16},{32,24},{40,32},{48,40},{56,48},{64,56},{72,6... | collective-permute-start | bytes 196616 | tf_op jit(solution)/shard_map/ppermute | solution.py:12
  50.6 12.2 %collective-permute-start.4 = (bf16[8,4096]{1,0:T(8,128)(2,1)}, bf16[8,4096]{1,0:T(8,128)(2,1)S(1)}, u32[]{:S(2)}, u32[]{:S(2)}) collective-permute-start(bf16[8,4096]{1,0:T(8,128)(2,1)} %fusion.62), channel_id=1, source_target_pairs={{8,0},{16,8},{24,16},{32,24},{40,32},{48,40},{56,48},{64,56},{72,6... | collective-permute-start | bytes 196616 | tf_op jit(solution)/shard_map/ppermute | solution.py:12
  53.2 0.8 copy-start.4
  54.0 0.7 copy-start.6
  56.5 5.6 %copy-start.12 = (bf16[8,4096]{1,0:T(8,128)(2,1)}, bf16[8,4096]{1,0:T(8,128)(2,1)S(1)}, u32[]{:S(2)}) copy-start(bf16[8,4096]{1,0:T(8,128)(2,1)S(1)} %collective-permute-done) | copy-start | bytes 196612
  57.4 4.7 %copy-start.14 = (bf16[8,4096]{1,0:T(8,128)(2,1)}, bf16[8,4096]{1,0:T(8,128)(2,1)S(1)}, u32[]{:S(2)}) copy-start(bf16[8,4096]{1,0:T(8,128)(2,1)S(1)} %collective-permute-done.1) | copy-start | bytes 196612
  60.1 0.8 copy-start.8
  61.6 1.8 copy-start.18
  72.9 107.2 %reduce-scatter.3.cloned.1.call-start = ((), (), s32[]{:S(2)}) async-start(), calls=%async_computation.2 | async-start | bytes 1179648 | tf_op jit(solution)/shard_map/reduce_scatter | solution.py:157
  75.3 6.3 %copy-start.7 = (bf16[48,32,128]{2,0,1:T(8,128)(2,1)S(1)}, bf16[48,32,128]{2,0,1:T(8,128)(2,1)}, u32[]{:S(2)}) copy-start(bf16[48,32,128]{2,0,1:T(8,128)(2,1)} %get-tuple-element.29) | copy-start | bytes 1179652
  76.4 14.6 %collective-permute-start.7 = (bf16[8,4096]{1,0:T(8,128)(2,1)}, bf16[8,4096]{1,0:T(8,128)(2,1)}, u32[]{:S(2)}, u32[]{:S(2)}) collective-permute-start(bf16[8,4096]{1,0:T(8,128)(2,1)} %fusion.60), channel_id=1, source_target_pairs={{8,0},{16,8},{24,16},{32,24},{40,32},{48,40},{56,48},{64,56},{72,6... | collective-permute-start | bytes 196616 | tf_op jit(solution)/shard_map/ppermute | solution.py:12
  83.2 7.8 %collective-permute-start.5 = (bf16[8,4096]{1,0:T(8,128)(2,1)S(1)}, bf16[8,4096]{1,0:T(8,128)(2,1)S(1)}, u32[]{:S(2)}, u32[]{:S(2)}) collective-permute-start(bf16[8,4096]{1,0:T(8,128)(2,1)S(1)} %fusion.61), channel_id=1, source_target_pairs={{8,0},{16,8},{24,16},{32,24},{40,32},{48,40},{56,48},{64,56},{72,6... | collective-permute-start | bytes 196616 | tf_op jit(solution)/shard_map/ppermute | solution.py:12
  85.7 1.3 copy-start.13
  85.8 1.3 copy-start.15
  87.1 9.9 %collective-permute-start.2 = (bf16[8,4096]{1,0:T(8,128)(2,1)S(1)}, bf16[8,4096]{1,0:T(8,128)(2,1)S(1)}, u32[]{:S(2)}, u32[]{:S(2)}) collective-permute-start(bf16[8,4096]{1,0:T(8,128)(2,1)S(1)} %get-tuple-element.41), channel_id=1, source_target_pairs={{1016,0},{0,8},{8,16},{16,24},{24,32},{32,40},{40,48},{48,56},{56,... | collective-permute-start | bytes 196616 | tf_op jit(solution)/shard_map/ppermute | solution.py:12
  89.1 9.2 %collective-permute-start.6 = (bf16[8,4096]{1,0:T(8,128)(2,1)S(1)}, bf16[8,4096]{1,0:T(8,128)(2,1)S(1)}, u32[]{:S(2)}, u32[]{:S(2)}) collective-permute-start(bf16[8,4096]{1,0:T(8,128)(2,1)S(1)} %get-tuple-element.40), channel_id=1, source_target_pairs={{1016,0},{0,8},{8,16},{16,24},{24,32},{32,40},{40,48},{48,56},{56,... | collective-permute-start | bytes 196616 | tf_op jit(solution)/shard_map/ppermute | solution.py:12
Sparse Core Ops, SparseCore 0:
  73.0 46.9 reduce-scatter.4
  123.9 56.0 reduce-scatter.2
where the time goes:
time: 193 us; the launch traced here: 190 us
  waiting for transfers between devices  89.1 us (46%)
  starting transfers between devices  38.7 us (20%)
  local copies, waits for them, and re-layouts  25.3 us (13%)
  between operations  18.3 us (9%)
  matrix products  9.99 us (5%)
  other arithmetic  8.83 us (5%)
    reduce_scatter x1, waiting for transfers between devices, on_device(): lax.psum_scatter(up_term.astype(jnp.bfloat16), 'dp', scatter_dimension=0,...  60.1 us
    ppermute x8, starting transfers between devices, from_behind(): return lax.ppermute(block, axis, route)  38.6 us
    reduce_scatter x1, waiting for transfers between devices, on_device(): lax.psum_scatter(down_term.astype(jnp.bfloat16), 'dp', scatter_dimension=...  21.7 us
    unnamed x67, local copies, waits for them, and re-layouts  16.2 us
    ppermute x8, waiting for transfers between devices, from_behind(): return lax.ppermute(block, axis, route)  7.26 us
    dot_general x2, matrix products, grad_blocks(): jnp.einsum('rnk,rnj->nkj', picked, cot_part, preferred_element_type=jnp.f...  4.12 us
  transfers between devices with their start and end apart: 10, of which 4 were waited for; matrix products, arithmetic and copies ran while one was open for 9% of the time, Pallas kernels for 0%

commit v1 on v0

v1 whole, which is shorter than its diff:
```python
import functools

import jax
import jax.numpy as jnp
from jax import lax
from jax.experimental import pallas as pl
from jax.experimental.pallas import tpu as pltpu
from jax.sharding import PartitionSpec as P

BLOCK = 128
UNROLL = 8
MESH = pl.DeviceIdType.MESH
F32 = jnp.float32
BF16 = jnp.bfloat16


def logistic(z):
    return 0.5 * jnp.tanh(0.5 * z) + 0.5


def silu_of(z, sig):
    return z * sig


def slope_of(z, sig):
    return sig * (1.0 + z * (1.0 - sig))


def curve_of(z, sig):
    return sig * (1.0 - sig) * (2.0 + z * (1.0 - 2.0 * sig))


def cols(i, width=BLOCK):
    return pl.ds(pl.multiple_of(i * width, width), width)


def each_block(count, body):
    def step(t, carry):
        for u in range(UNROLL):
            body(t * UNROLL + u)
        return carry

    lax.fori_loop(0, count // UNROLL, step, 0)


def dot(a, b):
    return jnp.dot(a, b, preferred_element_type=F32)


def dot_t(a, b):
    return lax.dot_general(a, b, (((1,), (1,)), ((), ())), preferred_element_type=F32)


def tick_kernel(
    n_section, n_dp, blocks, scale,
    up_index, down_index, tick_order, links,
    w_up, w_down, values_in, score_in, tangent_in, adjoint_in,
    saved_back, saved_tan, saved_second, saved_second_tan, saved_second_grad,
    vt_out, ga_out, grads_out,
    wu, wd, raw_x, raw_v, raw_c, x_slots, c_slots, xt, xs, cs,
    v0, v1, g1, v_sent, g_sent, v_last, g_last,
    ys, yy, e0, e1, h0, h1, rx, ry, rc, re,
    chain, chain2, keep,
    in_sem, send_sem, recv_sem, link_send, link_recv,
):
    section = lax.axis_index("section")
    me = lax.axis_index("dp")
    after = lax.rem(section + 1, n_section)
    before = lax.rem(section + n_section - 1, n_section)
    kept = blocks // n_dp

    loads = []

    def load(source, target):
        copy = pltpu.make_async_copy(source, target, in_sem.at[len(loads)])
        copy.start()
        loads.append(copy)

    for slot in range(2):
        for at, saved in enumerate((saved_back, saved_second, saved_second_tan, saved_tan)):
            load(saved.at[0, slot], raw_x.at[slot, pl.ds(8 * at, 8)])
    load(score_in.at[0], raw_c.at[pl.ds(0, 8)])
    load(adjoint_in.at[0], raw_c.at[pl.ds(8, 8)])
    for slot in range(2):
        load(saved_second_grad.at[0, slot], raw_c.at[pl.ds(16 + 8 * slot, 8)])
    early = len(loads)
    load(values_in.at[0], raw_v.at[pl.ds(0, 8)])
    load(tangent_in.at[0], raw_v.at[pl.ds(8, 8)])
    load(w_down.at[0], wd)
    load(w_up.at[0], wu)

    barrier = pltpu.get_barrier_semaphore()
    for p in range(1, n_dp):
        pl.semaphore_signal(barrier, inc=1, device_id={"dp": lax.rem(me + p, n_dp)}, device_id_type=MESH)
    for s in (after, before):
        pl.semaphore_signal(barrier, inc=1, device_id={"section": s}, device_id_type=MESH)

    first = tick_order[0, 0] * blocks
    later = tick_order[0, 1] * blocks

    chain[0] = jnp.zeros(chain.shape[1:], F32)
    chain2[0] = jnp.zeros(chain2.shape[1:], F32)

    for copy in loads[:early]:
        copy.wait()

    def to_blocks(j):
        here = cols(j)
        for slot in range(2):
            x_slots[slot * blocks + j] = raw_x[slot, :, here]
            c_slots[slot * blocks + j] = raw_c[pl.ds(16 + 8 * slot, 8), here]
        cs[j, pl.ds(0, 16)] = raw_c[pl.ds(0, 16), here]

    each_block(blocks, to_blocks)

    def gather_x(j):
        source = up_index[0, j]
        xs[j, pl.ds(0, 24)] = x_slots[first + source, pl.ds(0, 24)]
        xs[j, pl.ds(24, 8)] = x_slots[later + source, pl.ds(16, 8)]
        xs[j, pl.ds(32, 16)] = x_slots[later + source, pl.ds(0, 16)]
        cs[j, pl.ds(16, 8)] = c_slots[first + j]
        cs[j, pl.ds(24, 8)] = c_slots[later + j]

    each_block(blocks, gather_x)
    pl.semaphore_wait(barrier, n_dp + 1)

    sent = []

    def slab(ref, d):
        return ref.at[pl.ds(d * kept, kept)]

    def spread(kind, source, landing):
        for p in range(1, n_dp):
            peer = lax.rem(me + p, n_dp)
            copy = pltpu.make_async_remote_copy(
                src_ref=slab(source, peer),
                dst_ref=landing(me),
                send_sem=send_sem.at[kind, p - 1],
                recv_sem=recv_sem.at[kind, p - 1],
                device_id={"dp": peer},
                device_id_type=MESH,
            )
            copy.start()
            sent.append(copy)

    spread(0, xs, lambda d: rx.at[d])
    spread(1, cs, lambda d: rc.at[d, :, pl.ds(0, 32)])
    rx[me] = xs[pl.ds(me * kept, kept)]
    rc[me, :, pl.ds(0, 32)] = cs[pl.ds(me * kept, kept)]

    for copy in loads[early : early + 2]:
        copy.wait()

    def to_blocks_v(j):
        v0[j] = raw_v[:, cols(j)]

    each_block(blocks, to_blocks_v)

    def gather_v(j):
        source = up_index[0, j]
        xt[j, pl.ds(0, 16)] = v0[source]
        xt[j, pl.ds(16, 8)] = x_slots[first + source, pl.ds(24, 8)]
        xt[j, pl.ds(24, 8)] = x_slots[later + source, pl.ds(24, 8)]

    each_block(blocks, gather_v)
    loads[early + 2].wait()

    def pull(i):
        chain[i + 1] = dot_t(cs[i], wd[i]) + chain[links[0, i]]

    each_block(blocks, pull)
    loads[early + 3].wait()

    def raise_all(j):
        z = dot(jnp.concatenate([xt[j], xs[j]], 0), wu[j])
        zv, zt, tan_f, tan_l = z[0:8], z[8:16], z[16:24], z[24:32]
        back_f, za_f, ta_f = z[32:40], z[40:48], z[48:56]
        ta_l, back_l, za_l = z[56:64], z[64:72], z[72:80]
        pulled = chain[links[2, j]]
        pg, pa, ps_f, ps_l = pulled[0:8], pulled[8:16], pulled[16:24], pulled[24:32]
        sig_f, sig_l = logistic(za_f), logistic(za_l)
        slope_f, slope_l = slope_of(za_f, sig_f), slope_of(za_l, sig_l)
        sig_bf, sig_bl = logistic(back_f), logistic(back_l)
        hidden = silu_of(zv, logistic(zv))
        tangent_hidden = slope_of(tan_f, logistic(tan_f)) * zt
        h0[j] = jnp.concatenate([hidden, tangent_hidden], 0).astype(BF16)
        gate = slope_of(back_f, sig_bf) * pg
        push = slope_f * pa + curve_of(za_f, sig_f) * ps_f * ta_f
        e0[j] = jnp.concatenate([gate, push, slope_f * ps_f, slope_l * ps_l], 0).astype(BF16)
        yy[j] = jnp.concatenate(
            [
                silu_of(back_f, sig_bf),
                silu_of(za_f, sig_f),
                slope_f * ta_f,
                slope_l * ta_l,
                silu_of(back_l, sig_bl),
                silu_of(za_l, sig_l),
            ],
            0,
        ).astype(BF16)
        keep[j] = jnp.concatenate(
            [
                slope_of(back_l, sig_bl),
                slope_l,
                curve_of(za_l, sig_l) * ps_l * ta_l,
                slope_of(tan_l, logistic(tan_l)),
            ],
            0,
        )

    each_block(blocks, raise_all)

    def push_back(source):
        def body(j):
            chain2[j + 1] = dot_t(source[j, pl.ds(0, 16)], wu[j]) + chain2[links[1, j]]

        each_block(blocks, body)

    def settle(source, put):
        def body(b):
            put(b, (source[b, pl.ds(0, 16)].astype(F32) + chain2[links[3, b]]).astype(BF16))

        each_block(blocks, body)

    def lower(hidden, source, put):
        def body(i):
            put(i, (source[i].astype(F32) + dot(hidden[down_index[0, i]], wd[i])).astype(BF16))

        each_block(blocks, body)

    def in_block(ref):
        def put(i, value):
            ref[i] = value

        return put

    def in_rows(ref):
        def put(i, value):
            ref[:, cols(i)] = value

        return put

    def relay(kind, source, landing, to):
        copy = pltpu.make_async_remote_copy(
            src_ref=source,
            dst_ref=landing,
            send_sem=link_send.at[kind],
            recv_sem=link_recv.at[kind],
            device_id={"section": to},
            device_id_type=MESH,
        )
        copy.start()
        return copy

    push_back(e0)
    settle(cs, in_block(g_sent))
    g_copy = relay(0, g_sent, g1, before)
    lower(h0, v0, in_block(v_sent))
    v_copy = relay(1, v_sent, v1, after)

    def gather_y(i):
        ys[i] = yy[down_index[0, i]]

    each_block(blocks, gather_y)
    spread(2, ys, lambda d: ry.at[d])
    spread(3, e0, lambda d: re.at[d, :, pl.ds(0, 32)])
    ry[me] = ys[pl.ds(me * kept, kept)]
    re[me, :, pl.ds(0, 32)] = e0[pl.ds(me * kept, kept)]

    g_copy.wait_recv()
    spread(4, g1, lambda d: rc.at[d, :, pl.ds(32, 16)])
    rc[me, :, pl.ds(32, 16)] = g1[pl.ds(me * kept, kept)]

    def pull_later(i):
        chain[i + 1, pl.ds(0, 16)] = dot_t(g1[i], wd[i]) + chain[links[0, i], pl.ds(0, 16)]

    each_block(blocks, pull_later)

    def gate_later(j):
        pulled = chain[links[2, j], pl.ds(0, 16)]
        kept_rows = keep[j]
        gate = kept_rows[0:8] * pulled[0:8]
        push = kept_rows[8:16] * pulled[8:16] + kept_rows[16:24]
        e1[j] = jnp.concatenate([gate, push], 0).astype(BF16)

    each_block(blocks, gate_later)
    spread(5, e1, lambda d: re.at[d, :, pl.ds(32, 16)])
    re[me, :, pl.ds(32, 16)] = e1[pl.ds(me * kept, kept)]

    push_back(e1)
    settle(g1, in_rows(g_last))
    g_end = relay(2, g_last, ga_out, before)

    v_copy.wait_recv()

    def raise_later(j):
        z = dot(v1[up_index[0, j]], wu[j])
        zv, zt = z[0:8], z[8:16]
        h1[j] = jnp.concatenate([silu_of(zv, logistic(zv)), keep[j, pl.ds(24, 8)] * zt], 0).astype(BF16)

    each_block(blocks, raise_later)
    lower(h1, v1, in_rows(v_last))
    v_end = relay(3, v_last, vt_out, after)

    for copy in sent:
        copy.wait_recv()

    def rows_of(ref, k):
        return ref[:, k].reshape(n_dp * 48, BLOCK)

    for k in range(kept):
        for half, (left, right) in enumerate(((rx, re), (ry, rc))):
            grad = lax.dot_general(
                rows_of(left, k), rows_of(right, k), (((0,), (0,)), ((), ())), preferred_element_type=F32
            )
            grads_out[half, k] = (grad * scale).astype(BF16)

    for copy in sent:
        copy.wait_send()
    g_copy.wait_send()
    v_copy.wait_send()
    g_end.wait()
    v_end.wait()


def hand_out(vt, ga, grads, values, score, tangent, adjoint, up, down):
    values[0] = vt[pl.ds(0, 8)]
    tangent[0] = vt[pl.ds(8, 8)]
    score[0] = ga[pl.ds(0, 8)]
    adjoint[0] = ga[pl.ds(8, 8)]
    up[0] = grads[0]
    down[0] = grads[1]


def chain_links(down_index, up_index):
    index = jnp.concatenate([down_index, up_index], 0)
    count = index.shape[1]
    spot = jnp.arange(count, dtype=jnp.int32)
    own = jnp.concatenate([index, jnp.broadcast_to(spot, index.shape)], 0)
    over = jnp.concatenate([index, index], 0)
    limit = jnp.where(jnp.arange(4)[:, None] < 2, spot[None], count)
    hit = (own[:, :, None] == over[:, None, :]) & (spot[None, None, :] < limit[:, :, None])
    return jnp.max(jnp.where(hit, spot[None, None, :] + 1, 0), axis=2).astype(jnp.int32)


def on_device(mesh_shape, *arrays):
    (w_up, up_index, w_down, down_index, tick_order, *rest) = arrays
    n_section, n_dp = mesh_shape["section"], mesh_shape["dp"]
    blocks = w_up.shape[1]
    rows, width = rest[0].shape[1:]
    kept = blocks // n_dp
    links = chain_links(down_index, up_index)
    smem = pl.BlockSpec(memory_space=pltpu.SMEM)
    anywhere = pl.BlockSpec(memory_space=pl.ANY)
    vmem = pl.BlockSpec(memory_space=pltpu.VMEM)

    def by_block(height, copies=1):
        return pltpu.VMEM((copies * blocks, height, BLOCK), BF16)

    vt, ga, grads = pl.pallas_call(
        functools.partial(tick_kernel, n_section, n_dp, blocks, 1.0 / (rows * n_dp)),
        out_shape=(
            jax.ShapeDtypeStruct((16, width), BF16),
            jax.ShapeDtypeStruct((16, width), BF16),
            jax.ShapeDtypeStruct((2, kept, BLOCK, BLOCK), BF16),
        ),
        in_specs=[smem] * 4 + [anywhere] * 11,
        out_specs=(anywhere, anywhere, vmem),
        scratch_shapes=[
            pltpu.VMEM((blocks, BLOCK, BLOCK), BF16),
            pltpu.VMEM((blocks, BLOCK, BLOCK), BF16),
            pltpu.VMEM((2, 32, width), BF16),
            pltpu.VMEM((16, width), BF16),
            pltpu.VMEM((32, width), BF16),
            by_block(32, 2),
            by_block(8, 2),
            by_block(32),
            by_block(48),
            by_block(32),
            *[by_block(16)] * 5,
            *[pltpu.VMEM((16, width), BF16)] * 2,
            by_block(48),
            by_block(48),
            by_block(32),
            *[by_block(16)] * 3,
            *[pltpu.VMEM((n_dp, kept, 48, BLOCK), BF16)] * 4,
            pltpu.VMEM((blocks + 1, 32, BLOCK), F32),
            pltpu.VMEM((blocks + 1, 16, BLOCK), F32),
            pltpu.VMEM((blocks, 32, BLOCK), F32),
            pltpu.SemaphoreType.DMA((16,)),
            pltpu.SemaphoreType.DMA((6, n_dp - 1)),
            pltpu.SemaphoreType.DMA((6, n_dp - 1)),
            pltpu.SemaphoreType.DMA((4,)),
            pltpu.SemaphoreType.DMA((4,)),
        ],
        compiler_params=pltpu.CompilerParams(
            collective_id=0, has_side_effects=True, vmem_limit_bytes=40 << 20
        ),
        name="ticks",
    )(up_index, down_index, tick_order, links, w_up, w_down, *rest)
    stream = jax.ShapeDtypeStruct((1, rows, width), BF16)
    grad = jax.ShapeDtypeStruct((1, kept, BLOCK, BLOCK), BF16)
    return pl.pallas_call(
        hand_out,
        out_shape=(stream,) * 4 + (grad,) * 2,
        in_specs=[vmem] * 3,
        out_specs=(vmem,) * 6,
        name="hand_out",
    )(vt, ga, grads)


def solution(mesh):
    matrix = P("section", None, None, None)
    table = P("section", None)
    stream = P("section", "dp", None)
    saved = P("section", None, "dp", None)
    return jax.shard_map(
        functools.partial(on_device, dict(mesh.shape)),
        mesh=mesh,
        in_specs=(matrix, table, matrix, table, table) + (stream,) * 4 + (saved,) * 5,
        out_specs=(stream,) * 4 + (P("section", "dp", None, None),) * 2,
        check_vma=False,
    )
```

time: 193 us -> 58.5 us (0.30); the launches traced: 190 us -> 57.8 us
  waiting for transfers between devices: 89.1 us -> 0 us
  Pallas kernels: 0 us -> 43.4 us
  starting transfers between devices: 38.7 us -> 0 us
  between operations: 18.3 us -> 0.7 us
  local copies, waits for them, and re-layouts: 25.3 us -> 13.4 us
  matrix products: 9.99 us -> 0 us
  other arithmetic: 8.83 us -> 0.32 us
    reduce_scatter x2 -> x0, waiting for transfers between devices: 81.8 us -> none  [the longest x1 60.1 us: on_device(): lax.psum_scatter(up_term.astype(jnp.bfloat16), 'dp', scatter_dimension=0,...]
    pallas_call x0 -> x2, Pallas kernels: none -> 43.4 us  [the longest x1 41.5 us: on_device(): pl.pallas_call(functools.partial(tick_kernel, n_section, n_dp, blocks, 1....]
    ppermute x8 -> x0, starting transfers between devices: 38.6 us -> none  [from_behind(): return lax.ppermute(block, axis, route)]
    dot_general x18 -> x0, matrix products: 9.99 us -> none  [the longest x2 4.12 us: grad_blocks(): jnp.einsum('rnk,rnj->nkj', picked, cot_part, preferred_element_type=jnp.f...]
    ppermute x8 -> x0, waiting for transfers between devices: 7.26 us -> none  [from_behind(): return lax.ppermute(block, axis, route)]
    gather x6 -> x0, local copies, waits for them, and re-layouts: 6.3 us -> none  [the longest x2 3.48 us: grad_blocks(): picked = jnp.take(pieces, block_table, axis=1)]
    convert_element_type x8 -> x0, other arithmetic: 3.11 us -> none  [the longest x2 1.42 us: on_device(): (adjoint.astype(jnp.float32) + returned_adjoint).astype(jnp.bfloat16)]
    unnamed x67 -> x34, local copies, waits for them, and re-layouts: 16.2 us -> 13.4 us
  transfers between devices with their start and end apart: 10 -> 0, of which waited for: 4 -> 0; matrix products, arithmetic and copies ran while one was open for 9% -> 0% of each run, Pallas kernels for 0% -> 0%
where the time goes in v1:
time: 58.5 us; the launch traced here: 57.8 us
  Pallas kernels  43.4 us (74%)
  local copies, waits for them, and re-layouts  13.4 us (23%)
  between operations  0.7 us (1%)
    pallas_call x1, Pallas kernels, on_device(): pl.pallas_call(functools.partial(tick_kernel, n_section, n_dp, blocks, 1....  41.5 us
    unnamed x34, local copies, waits for them, and re-layouts  13.4 us
    pallas_call x1, Pallas kernels, on_device(): pl.pallas_call(hand_out, out_shape=(stream,) * 4 + (grad,) * 2, in_specs=...  1.87 us

profile of v1, /device:TPU:6, one launch (start us, length us, event | category | flops | bytes accessed | tf_op | source)
XLA Modules:
  0.0 57.8 jit_solution(4410214439672424875)
XLA Ops:
  0.7 0.0 copy-start.14
  0.7 0.0 copy-start.15
  0.7 0.6 %copy-done.14 = s32[1,32]{1,0:T(1,128)S(1)} copy-done((s32[1,32]{1,0:T(1,128)S(1)}, s32[1,32]{1,0:T(1,128)}, u32[]{:S(2)}) %copy-start.14) | copy-done | bytes 152
  1.3 0.0 copy-done.15
  1.3 0.1 pad_add_fusion
  1.4 0.0 copy-start.16
  1.4 0.2 select_reduce_fusion.links
  1.6 0.4 copy-done.16
  2.1 0.0 copy-start
  2.1 1.2 %copy-done = bf16[1,32,128,128]{3,2,1,0:T(8,128)(2,1)S(1)} copy-done((bf16[1,32,128,128]{3,2,1,0:T(8,128)(2,1)S(1)}, bf16[1,32,128,128]{3,2,1,0:T(8,128)(2,1)}, u32[]{:S(2)}) %copy-start) | copy-done | bytes 1048600
  3.3 0.0 copy-start.1
  3.3 1.2 %copy-done.1 = bf16[1,32,128,128]{3,2,1,0:T(8,128)(2,1)S(1)} copy-done((bf16[1,32,128,128]{3,2,1,0:T(8,128)(2,1)S(1)}, bf16[1,32,128,128]{3,2,1,0:T(8,128)(2,1)}, u32[]{:S(2)}) %copy-start.1) | copy-done | bytes 1048600
  4.5 0.0 copy-start.5
  4.5 0.9 %copy-done.5 = bf16[1,2,8,4096]{3,2,1,0:T(8,128)(2,1)S(1)} copy-done((bf16[1,2,8,4096]{3,2,1,0:T(8,128)(2,1)S(1)}, bf16[1,2,8,4096]{3,2,1,0:T(8,128)(2,1)}, u32[]{:S(2)}) %copy-start.5) | copy-done | bytes 131096
  5.4 0.0 copy-start.6
  5.4 0.9 %copy-done.6 = bf16[1,2,8,4096]{3,2,1,0:T(8,128)(2,1)S(1)} copy-done((bf16[1,2,8,4096]{3,2,1,0:T(8,128)(2,1)S(1)}, bf16[1,2,8,4096]{3,2,1,0:T(8,128)(2,1)}, u32[]{:S(2)}) %copy-start.6) | copy-done | bytes 131096
  6.3 0.0 copy-start.7
  6.3 0.9 %copy-done.7 = bf16[1,2,8,4096]{3,2,1,0:T(8,128)(2,1)S(1)} copy-done((bf16[1,2,8,4096]{3,2,1,0:T(8,128)(2,1)S(1)}, bf16[1,2,8,4096]{3,2,1,0:T(8,128)(2,1)}, u32[]{:S(2)}) %copy-start.7) | copy-done | bytes 131096
  7.2 0.0 copy-start.8
  7.2 0.9 %copy-done.8 = bf16[1,2,8,4096]{3,2,1,0:T(8,128)(2,1)S(1)} copy-done((bf16[1,2,8,4096]{3,2,1,0:T(8,128)(2,1)S(1)}, bf16[1,2,8,4096]{3,2,1,0:T(8,128)(2,1)}, u32[]{:S(2)}) %copy-start.8) | copy-done | bytes 131096
  8.1 0.0 copy-start.9
  8.1 0.9 %copy-done.9 = bf16[1,2,8,4096]{3,2,1,0:T(8,128)(2,1)S(1)} copy-done((bf16[1,2,8,4096]{3,2,1,0:T(8,128)(2,1)S(1)}, bf16[1,2,8,4096]{3,2,1,0:T(8,128)(2,1)}, u32[]{:S(2)}) %copy-start.9) | copy-done | bytes 131096
  9.0 0.0 copy-start.10
  9.0 0.8 %copy-done.10 = bf16[1,8,4096]{2,1,0:T(8,128)(2,1)S(1)} copy-done((bf16[1,8,4096]{2,1,0:T(8,128)(2,1)S(1)}, bf16[1,8,4096]{2,1,0:T(8,128)(2,1)}, u32[]{:S(2)}) %copy-start.10) | copy-done | bytes 65560
  9.9 0.0 copy-start.11
  9.9 0.8 %copy-done.11 = bf16[1,8,4096]{2,1,0:T(8,128)(2,1)S(1)} copy-done((bf16[1,8,4096]{2,1,0:T(8,128)(2,1)S(1)}, bf16[1,8,4096]{2,1,0:T(8,128)(2,1)}, u32[]{:S(2)}) %copy-start.11) | copy-done | bytes 65560
  10.7 0.0 copy-start.12
  10.7 0.8 %copy-done.12 = bf16[1,8,4096]{2,1,0:T(8,128)(2,1)S(1)} copy-done((bf16[1,8,4096]{2,1,0:T(8,128)(2,1)S(1)}, bf16[1,8,4096]{2,1,0:T(8,128)(2,1)}, u32[]{:S(2)}) %copy-start.12) | copy-done | bytes 65560
  11.6 0.0 copy-start.13
  11.6 0.8 %copy-done.13 = bf16[1,8,4096]{2,1,0:T(8,128)(2,1)S(1)} copy-done((bf16[1,8,4096]{2,1,0:T(8,128)(2,1)S(1)}, bf16[1,8,4096]{2,1,0:T(8,128)(2,1)}, u32[]{:S(2)}) %copy-start.13) | copy-done | bytes 65560
  12.4 41.5 %ticks.1 = (bf16[16,4096]{1,0:T(8,128)(2,1)S(1)}, bf16[16,4096]{1,0:T(8,128)(2,1)S(1)}, bf16[2,4,128,128]{3,2,1,0:T(8,128)(2,1)S(1)}) custom-call(s32[1,32]{1,0:T(1,128)S(1)} %copy-done.14, s32[1,32]{1,0:T(1,128)S(1)} %copy-done.15, s32[1,2]{1,0:T(1,128)S(1)} %copy-done.16, s32[4,32]{1,0:T(4,128)S(1)} %select_reduce_fusion.links, ...), custom_call_target="tpu_custom_call" | custom-call | tf_op jit(solution)/shard_map/ticks/pallas_call | solution.py:360
  53.9 0.0 copy-start.2
  53.9 0.7 %copy-done.2 = bf16[2,4,128,128]{3,2,1,0:T(8,128)(2,1)} copy-done((bf16[2,4,128,128]{3,2,1,0:T(8,128)(2,1)}, bf16[2,4,128,128]{3,2,1,0:T(8,128)(2,1)S(1)}, u32[]{:S(2)}) %copy-start.2) | copy-done | bytes 262168
  54.6 0.0 copy-start.3
  54.6 0.7 %copy-done.3 = bf16[16,4096]{1,0:T(8,128)(2,1)} copy-done((bf16[16,4096]{1,0:T(8,128)(2,1)}, bf16[16,4096]{1,0:T(8,128)(2,1)S(1)}, u32[]{:S(2)}) %copy-start.3) | copy-done | bytes 131096
  55.2 0.0 copy-start.4
  55.2 0.7 %copy-done.4 = bf16[16,4096]{1,0:T(8,128)(2,1)} copy-done((bf16[16,4096]{1,0:T(8,128)(2,1)}, bf16[16,4096]{1,0:T(8,128)(2,1)S(1)}, u32[]{:S(2)}) %copy-start.4) | copy-done | bytes 131096
  55.9 1.9 %hand_out.1 = (bf16[1,8,4096]{2,1,0:T(8,128)(2,1)}, bf16[1,8,4096]{2,1,0:T(8,128)(2,1)}, bf16[1,8,4096]{2,1,0:T(8,128)(2,1)}, bf16[1,8,4096]{2,1,0:T(8,128)(2,1)...) custom-call(bf16[16,4096]{1,0:T(8,128)(2,1)} %copy-done.3, bf16[16,4096]{1,0:T(8,128)(2,1)} %copy-done.4, ...), custom_call_target="tpu_custom_call" | custom-call | tf_op jit(solution)/shard_map/hand_out/pallas_call | solution.py:403
  (3 shorter events, 0.0 us)
Async XLA Ops:
  0.7 0.7 %copy-start.14 = (s32[1,32]{1,0:T(1,128)S(1)}, s32[1,32]{1,0:T(1,128)}, u32[]{:S(2)}) copy-start(s32[1,32]{1,0:T(1,128)} %up_index.1) | copy-start | bytes 388
  0.7 0.7 %copy-start.15 = (s32[1,32]{1,0:T(1,128)S(1)}, s32[1,32]{1,0:T(1,128)}, u32[]{:S(2)}) copy-start(s32[1,32]{1,0:T(1,128)} %down_index.1) | copy-start | bytes 388
  1.4 0.7 %copy-start.16 = (s32[1,2]{1,0:T(1,128)S(1)}, s32[1,2]{1,0:T(1,128)}, u32[]{:S(2)}) copy-start(s32[1,2]{1,0:T(1,128)} %tick_order.1) | copy-start | bytes 28
  2.1 1.2 %copy-start = (bf16[1,32,128,128]{3,2,1,0:T(8,128)(2,1)S(1)}, bf16[1,32,128,128]{3,2,1,0:T(8,128)(2,1)}, u32[]{:S(2)}) copy-start(bf16[1,32,128,128]{3,2,1,0:T(8,128)(2,1)} %w_up.1) | copy-start | bytes 3145732
  3.3 1.2 %copy-start.1 = (bf16[1,32,128,128]{3,2,1,0:T(8,128)(2,1)S(1)}, bf16[1,32,128,128]{3,2,1,0:T(8,128)(2,1)}, u32[]{:S(2)}) copy-start(bf16[1,32,128,128]{3,2,1,0:T(8,128)(2,1)} %w_down.1) | copy-start | bytes 3145732
  4.5 0.9 %copy-start.5 = (bf16[1,2,8,4096]{3,2,1,0:T(8,128)(2,1)S(1)}, bf16[1,2,8,4096]{3,2,1,0:T(8,128)(2,1)}, u32[]{:S(2)}) copy-start(bf16[1,2,8,4096]{3,2,1,0:T(8,128)(2,1)} %saved_back.1) | copy-start | bytes 393220
  5.4 0.9 %copy-start.6 = (bf16[1,2,8,4096]{3,2,1,0:T(8,128)(2,1)S(1)}, bf16[1,2,8,4096]{3,2,1,0:T(8,128)(2,1)}, u32[]{:S(2)}) copy-start(bf16[1,2,8,4096]{3,2,1,0:T(8,128)(2,1)} %saved_tan.1) | copy-start | bytes 393220
  6.3 0.9 %copy-start.7 = (bf16[1,2,8,4096]{3,2,1,0:T(8,128)(2,1)S(1)}, bf16[1,2,8,4096]{3,2,1,0:T(8,128)(2,1)}, u32[]{:S(2)}) copy-start(bf16[1,2,8,4096]{3,2,1,0:T(8,128)(2,1)} %saved_second.1) | copy-start | bytes 393220
  7.2 0.9 %copy-start.8 = (bf16[1,2,8,4096]{3,2,1,0:T(8,128)(2,1)S(1)}, bf16[1,2,8,4096]{3,2,1,0:T(8,128)(2,1)}, u32[]{:S(2)}) copy-start(bf16[1,2,8,4096]{3,2,1,0:T(8,128)(2,1)} %saved_second_tan.1) | copy-start | bytes 393220
  8.1 0.9 %copy-start.9 = (bf16[1,2,8,4096]{3,2,1,0:T(8,128)(2,1)S(1)}, bf16[1,2,8,4096]{3,2,1,0:T(8,128)(2,1)}, u32[]{:S(2)}) copy-start(bf16[1,2,8,4096]{3,2,1,0:T(8,128)(2,1)} %saved_second_grad.1) | copy-start | bytes 393220
  9.0 0.8 %copy-start.10 = (bf16[1,8,4096]{2,1,0:T(8,128)(2,1)S(1)}, bf16[1,8,4096]{2,1,0:T(8,128)(2,1)}, u32[]{:S(2)}) copy-start(bf16[1,8,4096]{2,1,0:T(8,128)(2,1)} %values_in.1) | copy-start | bytes 196612
  9.9 0.8 %copy-start.11 = (bf16[1,8,4096]{2,1,0:T(8,128)(2,1)S(1)}, bf16[1,8,4096]{2,1,0:T(8,128)(2,1)}, u32[]{:S(2)}) copy-start(bf16[1,8,4096]{2,1,0:T(8,128)(2,1)} %score_in.1) | copy-start | bytes 196612
  10.7 0.8 %copy-start.12 = (bf16[1,8,4096]{2,1,0:T(8,128)(2,1)S(1)}, bf16[1,8,4096]{2,1,0:T(8,128)(2,1)}, u32[]{:S(2)}) copy-start(bf16[1,8,4096]{2,1,0:T(8,128)(2,1)} %tangent_in.1) | copy-start | bytes 196612
  11.6 0.8 %copy-start.13 = (bf16[1,8,4096]{2,1,0:T(8,128)(2,1)S(1)}, bf16[1,8,4096]{2,1,0:T(8,128)(2,1)}, u32[]{:S(2)}) copy-start(bf16[1,8,4096]{2,1,0:T(8,128)(2,1)} %adjoint_in.1) | copy-start | bytes 196612
  53.9 0.7 %copy-start.2 = (bf16[2,4,128,128]{3,2,1,0:T(8,128)(2,1)}, bf16[2,4,128,128]{3,2,1,0:T(8,128)(2,1)S(1)}, u32[]{:S(2)}) copy-start(bf16[2,4,128,128]{3,2,1,0:T(8,128)(2,1)S(1)} %get-tuple-element.11.grads) | copy-start | bytes 786436
  54.6 0.7 %copy-start.3 = (bf16[16,4096]{1,0:T(8,128)(2,1)}, bf16[16,4096]{1,0:T(8,128)(2,1)S(1)}, u32[]{:S(2)}) copy-start(bf16[16,4096]{1,0:T(8,128)(2,1)S(1)} %get-tuple-element.9.vt) | copy-start | bytes 393220
  55.2 0.7 %copy-start.4 = (bf16[16,4096]{1,0:T(8,128)(2,1)}, bf16[16,4096]{1,0:T(8,128)(2,1)S(1)}, u32[]{:S(2)}) copy-start(bf16[16,4096]{1,0:T(8,128)(2,1)S(1)} %get-tuple-element.10.ga) | copy-start | bytes 393220

commit v2 on v1

--- a/solution.py
+++ b/solution.py
@@ -56,9 +56,9 @@
     up_index, down_index, tick_order, links,
     w_up, w_down, values_in, score_in, tangent_in, adjoint_in,
     saved_back, saved_tan, saved_second, saved_second_tan, saved_second_grad,
-    vt_out, ga_out, grads_out,
+    v_out, g_out, grads_out,
     wu, wd, raw_x, raw_v, raw_c, x_slots, c_slots, xt, xs, cs,
-    v0, v1, g1, v_sent, g_sent, v_last, g_last,
+    v0, v1, g1, v_sent, g_sent, v_last, g_last, grads,
     ys, yy, e0, e1, h0, h1, rx, ry, rc, re,
     chain, chain2, keep,
     in_sem, send_sem, recv_sem, link_send, link_recv,
@@ -236,7 +236,8 @@
 
     def in_rows(ref):
         def put(i, value):
-            ref[:, cols(i)] = value
+            ref[0, :, cols(i)] = value[0:8]
+            ref[1, :, cols(i)] = value[8:16]
 
         return put
 
@@ -289,7 +290,7 @@
 
     push_back(e1)
     settle(g1, in_rows(g_last))
-    g_end = relay(2, g_last, ga_out, before)
+    g_end = relay(2, g_last, g_out, before)
 
     v_copy.wait_recv()
 
@@ -300,7 +301,7 @@
 
     each_block(blocks, raise_later)
     lower(h1, v1, in_rows(v_last))
-    v_end = relay(3, v_last, vt_out, after)
+    v_end = relay(3, v_last, v_out, after)
 
     for copy in sent:
         copy.wait_recv()
@@ -313,23 +314,29 @@
             grad = lax.dot_general(
                 rows_of(left, k), rows_of(right, k), (((0,), (0,)), ((), ())), preferred_element_type=F32
             )
-            grads_out[half, k] = (grad * scale).astype(BF16)
-
+            grads[half, k] = (grad * scale).astype(BF16)
+
+    grad_copy = pltpu.make_async_copy(grads, grads_out, in_sem.at[len(loads)])
+    grad_copy.start()
     for copy in sent:
         copy.wait_send()
+    grad_copy.wait()
     g_copy.wait_send()
     v_copy.wait_send()
     g_end.wait()
     v_end.wait()
 
 
-def hand_out(vt, ga, grads, values, score, tangent, adjoint, up, down):
-    values[0] = vt[pl.ds(0, 8)]
-    tangent[0] = vt[pl.ds(8, 8)]
-    score[0] = ga[pl.ds(0, 8)]
-    adjoint[0] = ga[pl.ds(8, 8)]
-    up[0] = grads[0]
-    down[0] = grads[1]
+def hand_out(v, g, grads, values, score, tangent, adjoint, up, down, sem):
+    moves = ((v, 0, values), (v, 1, tangent), (g, 0, score), (g, 1, adjoint), (grads, 0, up), (grads, 1, down))
+    copies = [
+        pltpu.make_async_copy(source.at[half], target.at[0], sem.at[n])
+        for n, (source, half, target) in enumerate(moves)
+    ]
+    for copy in copies:
+        copy.start()
+    for copy in copies:
+        copy.wait()
 
 
 def chain_links(down_index, up_index):
@@ -351,21 +358,20 @@
     kept = blocks // n_dp
     links = chain_links(down_index, up_index)
     smem = pl.BlockSpec(memory_space=pltpu.SMEM)
-    anywhere = pl.BlockSpec(memory_space=pl.ANY)
-    vmem = pl.BlockSpec(memory_space=pltpu.VMEM)
+    hbm = pl.BlockSpec(memory_space=pltpu.HBM)
 
     def by_block(height, copies=1):
         return pltpu.VMEM((copies * blocks, height, BLOCK), BF16)
 
-    vt, ga, grads = pl.pallas_call(
+    v, g, grads = pl.pallas_call(
         functools.partial(tick_kernel, n_section, n_dp, blocks, 1.0 / (rows * n_dp)),
         out_shape=(
-            jax.ShapeDtypeStruct((16, width), BF16),
-            jax.ShapeDtypeStruct((16, width), BF16),
+            jax.ShapeDtypeStruct((2, rows, width), BF16),
+            jax.ShapeDtypeStruct((2, rows, width), BF16),
             jax.ShapeDtypeStruct((2, kept, BLOCK, BLOCK), BF16),
         ),
-        in_specs=[smem] * 4 + [anywhere] * 11,
-        out_specs=(anywhere, anywhere, vmem),
+        in_specs=[smem] * 4 + [hbm] * 11,
+        out_specs=(hbm, hbm, hbm),
         scratch_shapes=[
             pltpu.VMEM((blocks, BLOCK, BLOCK), BF16),
             pltpu.VMEM((blocks, BLOCK, BLOCK), BF16),
@@ -378,7 +384,8 @@
             by_block(48),
             by_block(32),
             *[by_block(16)] * 5,
-            *[pltpu.VMEM((16, width), BF16)] * 2,
+            *[pltpu.VMEM((2, 8, width), BF16)] * 2,
+            pltpu.VMEM((2, kept, BLOCK, BLOCK), BF16),
             by_block(48),
             by_block(48),
             by_block(32),
@@ -387,14 +394,14 @@
             pltpu.VMEM((blocks + 1, 32, BLOCK), F32),
             pltpu.VMEM((blocks + 1, 16, BLOCK), F32),
             pltpu.VMEM((blocks, 32, BLOCK), F32),
-            pltpu.SemaphoreType.DMA((16,)),
+            pltpu.SemaphoreType.DMA((17,)),
             pltpu.SemaphoreType.DMA((6, n_dp - 1)),
             pltpu.SemaphoreType.DMA((6, n_dp - 1)),
             pltpu.SemaphoreType.DMA((4,)),
             pltpu.SemaphoreType.DMA((4,)),
         ],
         compiler_params=pltpu.CompilerParams(
-            collective_id=0, has_side_effects=True, vmem_limit_bytes=40 << 20
+            collective_id=0, has_side_effects=True, vmem_limit_bytes=56 << 20
         ),
         name="ticks",
     )(up_index, down_index, tick_order, links, w_up, w_down, *rest)
@@ -403,10 +410,11 @@
     return pl.pallas_call(
         hand_out,
         out_shape=(stream,) * 4 + (grad,) * 2,
-        in_specs=[vmem] * 3,
-        out_specs=(vmem,) * 6,
+        in_specs=[hbm] * 3,
+        out_specs=(hbm,) * 6,
+        scratch_shapes=[pltpu.SemaphoreType.DMA((6,))],
         name="hand_out",
-    )(vt, ga, grads)
+    )(v, g, grads)
 
 
 def solution(mesh):

time: 58.5 us -> 60.1 us (1.027)
  Pallas kernels: 43.4 us -> 57.5 us
  local copies, waits for them, and re-layouts: 13.4 us -> 0.65 us
    pallas_call x1, Pallas kernels: 1.87 us -> 17 us  [on_device(): pl.pallas_call(hand_out, out_shape=(stream,) * 4 + (grad,) * 2, in_specs=...]
    unnamed x34 -> x4, local copies, waits for them, and re-layouts: 13.4 us -> 0.65 us
    pallas_call x1, Pallas kernels: 41.5 us -> 40.4 us  [on_device(): pl.pallas_call(functools.partial(tick_kernel, n_section, n_dp, blocks, 1....]
where the time goes in v2:
time: 60.1 us; the launch traced here: 59.7 us
  Pallas kernels  57.5 us (96%)
  other arithmetic  0.9 us (1%)
  between operations  0.68 us (1%)
  local copies, waits for them, and re-layouts  0.65 us (1%)
    pallas_call x1, Pallas kernels, on_device(): pl.pallas_call(functools.partial(tick_kernel, n_section, n_dp, blocks, 1....  40.4 us
    pallas_call x1, Pallas kernels, on_device(): pl.pallas_call(hand_out, out_shape=(stream,) * 4 + (grad,) * 2, in_specs=...  17 us

profile of v2, /device:TPU:6, one launch (start us, length us, event | category | flops | bytes accessed | tf_op | source)
XLA Modules:
  0.0 59.7 jit_solution(2251177859087739594)
XLA Ops:
  0.7 0.0 copy-start
  0.7 0.0 copy-start.1
  0.7 0.6 %copy-done = s32[1,32]{1,0:T(1,128)S(1)} copy-done((s32[1,32]{1,0:T(1,128)S(1)}, s32[1,32]{1,0:T(1,128)}, u32[]{:S(2)}) %copy-start) | copy-done | bytes 152
  1.3 0.0 copy-done.1
  1.3 0.1 pad_add_fusion
  1.4 0.8 %select_reduce_fusion.links = s32[4,32]{1,0:T(4,128)} fusion(s32[32]{0:T(128)S(1)} %iota_add_fusion, s32[4,32]{1,0:T(4,128)S(1)} %get-tuple-element.14, s32[4,32]{1,0:T(4,128)S(1)} %get-tuple-element.13, s32[4,32]{1,0:T(4,128)S(1)} %get-tuple-element.12), kind=kLoop, calls=%fused_computation | loop fusion | flops 20352 | bytes 2176 | tf_op jit(solution)/shard_map/reduce_max | solution.py:350
  2.2 40.4 %ticks.1 = (bf16[2,8,4096]{2,1,0:T(8,128)(2,1)}, bf16[2,8,4096]{2,1,0:T(8,128)(2,1)}, bf16[2,4,128,128]{3,2,1,0:T(8,128)(2,1)}) custom-call(s32[1,32]{1,0:T(1,128)} %up_index.1, s32[1,32]{1,0:T(1,128)} %down_index.1, s32[1,2]{1,0:T(1,128)} %tick_order.1, s32[4,32]{1,0:T(4,128)} %select_reduce_fusion.links, bf16[1,32,128,128]{3,2,1,0:T(8,128)(2,1)} %w_up.1, ...), custom_call_target="tpu_custom_call" | custom-call | tf_op jit(solution)/shard_map/ticks/pallas_call | solution.py:366
  42.7 17.0 %hand_out.1 = (bf16[1,8,4096]{2,1,0:T(8,128)(2,1)}, bf16[1,8,4096]{2,1,0:T(8,128)(2,1)}, bf16[1,8,4096]{2,1,0:T(8,128)(2,1)}, bf16[1,8,4096]{2,1,0:T(8,128)(2,1)...) custom-call(bf16[2,8,4096]{2,1,0:T(8,128)(2,1)} %get-tuple-element.9.v, ...), custom_call_target="tpu_custom_call" | custom-call | tf_op jit(solution)/shard_map/hand_out/pallas_call | solution.py:410
  (3 shorter events, 0.0 us)
Async XLA Ops:
  0.7 0.7 %copy-start = (s32[1,32]{1,0:T(1,128)S(1)}, s32[1,32]{1,0:T(1,128)}, u32[]{:S(2)}) copy-start(s32[1,32]{1,0:T(1,128)} %up_index.1) | copy-start | bytes 388
  0.7 0.7 %copy-start.1 = (s32[1,32]{1,0:T(1,128)S(1)}, s32[1,32]{1,0:T(1,128)}, u32[]{:S(2)}) copy-start(s32[1,32]{1,0:T(1,128)} %down_index.1) | copy-start | bytes 388

commit v3 on v2

--- a/solution.py
+++ b/solution.py
@@ -327,15 +327,25 @@
     v_end.wait()
 
 
-def hand_out(v, g, grads, values, score, tangent, adjoint, up, down, sem):
-    moves = ((v, 0, values), (v, 1, tangent), (g, 0, score), (g, 1, adjoint), (grads, 0, up), (grads, 1, down))
-    copies = [
-        pltpu.make_async_copy(source.at[half], target.at[0], sem.at[n])
-        for n, (source, half, target) in enumerate(moves)
+def hand_out(v, g, grads, values, score, tangent, adjoint, up, down, held, held_grads, in_sem, out_sem):
+    moves = (
+        (v, 0, values, held.at[0]),
+        (v, 1, tangent, held.at[1]),
+        (g, 0, score, held.at[2]),
+        (g, 1, adjoint, held.at[3]),
+        (grads, 0, up, held_grads.at[0]),
+        (grads, 1, down, held_grads.at[1]),
+    )
+    inward = [
+        pltpu.make_async_copy(source.at[half], stop, in_sem.at[n]) for n, (source, half, _, stop) in enumerate(moves)
     ]
-    for copy in copies:
+    outward = [pltpu.make_async_copy(stop, target.at[0], out_sem.at[n]) for n, (_, _, target, stop) in enumerate(moves)]
+    for copy in inward:
         copy.start()
-    for copy in copies:
+    for arrived, copy in zip(inward, outward):
+        arrived.wait()
+        copy.start()
+    for copy in outward:
         copy.wait()
 
 
@@ -412,7 +422,13 @@
         out_shape=(stream,) * 4 + (grad,) * 2,
         in_specs=[hbm] * 3,
         out_specs=(hbm,) * 6,
-        scratch_shapes=[pltpu.SemaphoreType.DMA((6,))],
+        scratch_shapes=[
+            pltpu.VMEM((4, rows, width), BF16),
+            pltpu.VMEM((2, kept, BLOCK, BLOCK), BF16),
+            pltpu.SemaphoreType.DMA((6,)),
+            pltpu.SemaphoreType.DMA((6,)),
+        ],
+        compiler_params=pltpu.CompilerParams(vmem_limit_bytes=56 << 20),
         name="hand_out",
     )(v, g, grads)
 

time: 60.1 us -> 45 us (0.75)
  Pallas kernels: 57.5 us -> 42.3 us
    pallas_call x1, Pallas kernels: 17 us -> 1.86 us  [on_device(): pl.pallas_call(hand_out, out_shape=(stream,) * 4 + (grad,) * 2, in_specs=...]
where the time goes in v3:
time: 45 us; the launch traced here: 44.5 us
  Pallas kernels  42.3 us (94%)
  other arithmetic  0.9 us (2%)
  between operations  0.68 us (2%)
  local copies, waits for them, and re-layouts  0.65 us (1%)
    pallas_call x1, Pallas kernels, on_device(): pl.pallas_call(functools.partial(tick_kernel, n_section, n_dp, blocks, 1....  40.4 us
    pallas_call x1, Pallas kernels, on_device(): pl.pallas_call(hand_out, out_shape=(stream,) * 4 + (grad,) * 2, in_specs=...  1.86 us

profile of v3, /device:TPU:6, one launch (start us, length us, event | category | flops | bytes accessed | tf_op | source)
XLA Modules:
  0.0 44.5 jit_solution(1975856287852812331)
XLA Ops:
  0.7 0.0 copy-start
  0.7 0.0 copy-start.1
  0.7 0.6 %copy-done = s32[1,32]{1,0:T(1,128)S(1)} copy-done((s32[1,32]{1,0:T(1,128)S(1)}, s32[1,32]{1,0:T(1,128)}, u32[]{:S(2)}) %copy-start) | copy-done | bytes 152
  1.3 0.0 copy-done.1
  1.3 0.1 pad_add_fusion
  1.4 0.8 %select_reduce_fusion.links = s32[4,32]{1,0:T(4,128)} fusion(s32[32]{0:T(128)S(1)} %iota_add_fusion, s32[4,32]{1,0:T(4,128)S(1)} %get-tuple-element.14, s32[4,32]{1,0:T(4,128)S(1)} %get-tuple-element.13, s32[4,32]{1,0:T(4,128)S(1)} %get-tuple-element.12), kind=kLoop, calls=%fused_computation | loop fusion | flops 20352 | bytes 2176 | tf_op jit(solution)/shard_map/reduce_max | solution.py:360
  2.2 40.4 %ticks.1 = (bf16[2,8,4096]{2,1,0:T(8,128)(2,1)}, bf16[2,8,4096]{2,1,0:T(8,128)(2,1)}, bf16[2,4,128,128]{3,2,1,0:T(8,128)(2,1)}) custom-call(s32[1,32]{1,0:T(1,128)} %up_index.1, s32[1,32]{1,0:T(1,128)} %down_index.1, s32[1,2]{1,0:T(1,128)} %tick_order.1, s32[4,32]{1,0:T(4,128)} %select_reduce_fusion.links, bf16[1,32,128,128]{3,2,1,0:T(8,128)(2,1)} %w_up.1, ...), custom_call_target="tpu_custom_call" | custom-call | tf_op jit(solution)/shard_map/ticks/pallas_call | solution.py:376
  42.7 1.9 %hand_out.1 = (bf16[1,8,4096]{2,1,0:T(8,128)(2,1)}, bf16[1,8,4096]{2,1,0:T(8,128)(2,1)}, bf16[1,8,4096]{2,1,0:T(8,128)(2,1)}, bf16[1,8,4096]{2,1,0:T(8,128)(2,1)...) custom-call(bf16[2,8,4096]{2,1,0:T(8,128)(2,1)} %get-tuple-element.9.v, ...), custom_call_target="tpu_custom_call" | custom-call | tf_op jit(solution)/shard_map/hand_out/pallas_call | solution.py:420
  (3 shorter events, 0.0 us)
Async XLA Ops:
  0.7 0.7 %copy-start = (s32[1,32]{1,0:T(1,128)S(1)}, s32[1,32]{1,0:T(1,128)}, u32[]{:S(2)}) copy-start(s32[1,32]{1,0:T(1,128)} %up_index.1) | copy-start | bytes 388
  0.7 0.7 %copy-start.1 = (s32[1,32]{1,0:T(1,128)S(1)}, s32[1,32]{1,0:T(1,128)}, u32[]{:S(2)}) copy-start(s32[1,32]{1,0:T(1,128)} %down_index.1) | copy-start | bytes 388

commit v4 on v3

--- a/solution.py
+++ b/solution.py
@@ -8,7 +8,9 @@
 from jax.sharding import PartitionSpec as P
 
 BLOCK = 128
-UNROLL = 8
+UNROLL = 32
+ALONG_X = (2, 1, 3)
+FAR_FIRST = ((2, 1), (2, 0), (1, 1), (1, 0), (3, 1), (3, 0), (0, 1))
 MESH = pl.DeviceIdType.MESH
 F32 = jnp.float32
 BF16 = jnp.bfloat16
@@ -35,16 +37,19 @@
 
 
 def each_block(count, body):
-    def step(t, carry):
-        for u in range(UNROLL):
-            body(t * UNROLL + u)
+    def step(i, carry):
+        body(i)
         return carry
 
-    lax.fori_loop(0, count // UNROLL, step, 0)
+    lax.fori_loop(0, count, step, 0, unroll=UNROLL)
 
 
 def dot(a, b):
     return jnp.dot(a, b, preferred_element_type=F32)
+
+
+def dot_rows(a, b):
+    return lax.dot_general(a, b, (((0,), (0,)), ((), ())), preferred_element_type=F32)
 
 
 def dot_t(a, b):
@@ -59,15 +64,18 @@
     v_out, g_out, grads_out,
     wu, wd, raw_x, raw_v, raw_c, x_slots, c_slots, xt, xs, cs,
     v0, v1, g1, v_sent, g_sent, v_last, g_last, grads,
-    ys, yy, e0, e1, h0, h1, rx, ry, rc, re,
+    ys, yy, e0, e1, h0, h1, xy, rx, rc, ry, re, rxy, rcl, rel, crossing, crossed, total,
     chain, chain2, keep,
-    in_sem, send_sem, recv_sem, link_send, link_recv,
+    in_sem, near_send, near_recv, send_sem, recv_sem, link_send, link_recv,
 ):
     section = lax.axis_index("section")
     me = lax.axis_index("dp")
     after = lax.rem(section + 1, n_section)
     before = lax.rem(section + n_section - 1, n_section)
     kept = blocks // n_dp
+    row = n_dp // 2
+    my_x, my_y = me % row, me // row
+    across = (1 - my_y) * row + my_x
 
     loads = []
 
@@ -117,7 +125,7 @@
         source = up_index[0, j]
         xs[j, pl.ds(0, 24)] = x_slots[first + source, pl.ds(0, 24)]
         xs[j, pl.ds(24, 8)] = x_slots[later + source, pl.ds(16, 8)]
-        xs[j, pl.ds(32, 16)] = x_slots[later + source, pl.ds(0, 16)]
+        xy[j, pl.ds(0, 16)] = x_slots[later + source, pl.ds(0, 16)]
         cs[j, pl.ds(16, 8)] = c_slots[first + j]
         cs[j, pl.ds(24, 8)] = c_slots[later + j]
 
@@ -126,27 +134,48 @@
 
     sent = []
 
+    near = []
+
     def slab(ref, d):
         return ref.at[pl.ds(d * kept, kept)]
 
+    def spread_near(*parts):
+        for side in (1, 0):
+            for kind, source, landing in parts:
+                for n, dx in enumerate(ALONG_X):
+                    x = (my_x + dx) % row
+                    peer = my_y * row + x
+                    keeper = (my_y if side == 0 else 1 - my_y) * row + x
+                    copy = pltpu.make_async_remote_copy(
+                        src_ref=slab(source, keeper),
+                        dst_ref=landing.at[side, my_x],
+                        send_sem=near_send.at[kind, side, n],
+                        recv_sem=near_recv.at[kind, side, n],
+                        device_id={"dp": peer},
+                        device_id_type=MESH,
+                    )
+                    copy.start()
+                    near.append((side, copy))
+        for kind, source, landing in parts:
+            landing[0, my_x] = source[pl.ds(me * kept, kept)]
+            landing[1, my_x] = source[pl.ds(across * kept, kept)]
+
     def spread(kind, source, landing):
-        for p in range(1, n_dp):
-            peer = lax.rem(me + p, n_dp)
+        for n, (dx, dy) in enumerate(FAR_FIRST):
+            peer = (my_y + dy) % 2 * row + (my_x + dx) % row
             copy = pltpu.make_async_remote_copy(
                 src_ref=slab(source, peer),
-                dst_ref=landing(me),
-                send_sem=send_sem.at[kind, p - 1],
-                recv_sem=recv_sem.at[kind, p - 1],
+                dst_ref=landing.at[me],
+                send_sem=send_sem.at[kind, n],
+                recv_sem=recv_sem.at[kind, n],
                 device_id={"dp": peer},
                 device_id_type=MESH,
             )
             copy.start()
             sent.append(copy)
-
-    spread(0, xs, lambda d: rx.at[d])
-    spread(1, cs, lambda d: rc.at[d, :, pl.ds(0, 32)])
-    rx[me] = xs[pl.ds(me * kept, kept)]
-    rc[me, :, pl.ds(0, 32)] = cs[pl.ds(me * kept, kept)]
+        landing[me] = source[pl.ds(me * kept, kept)]
+
+    spread_near((0, xs, rx), (1, cs, rc))
 
     for copy in loads[early : early + 2]:
         copy.wait()
@@ -172,7 +201,7 @@
     loads[early + 3].wait()
 
     def raise_all(j):
-        z = dot(jnp.concatenate([xt[j], xs[j]], 0), wu[j])
+        z = dot(jnp.concatenate([xt[j], xs[j], xy[j, pl.ds(0, 16)]], 0), wu[j])
         zv, zt, tan_f, tan_l = z[0:8], z[8:16], z[16:24], z[24:32]
         back_f, za_f, ta_f = z[32:40], z[40:48], z[48:56]
         ta_l, back_l, za_l = z[56:64], z[64:72], z[72:80]
@@ -260,17 +289,16 @@
     v_copy = relay(1, v_sent, v1, after)
 
     def gather_y(i):
-        ys[i] = yy[down_index[0, i]]
+        source = down_index[0, i]
+        ys[i] = yy[source, pl.ds(0, 32)]
+        xy[i, pl.ds(16, 16)] = yy[source, pl.ds(32, 16)]
 
     each_block(blocks, gather_y)
-    spread(2, ys, lambda d: ry.at[d])
-    spread(3, e0, lambda d: re.at[d, :, pl.ds(0, 32)])
-    ry[me] = ys[pl.ds(me * kept, kept)]
-    re[me, :, pl.ds(0, 32)] = e0[pl.ds(me * kept, kept)]
+    spread_near((2, ys, ry), (3, e0, re))
+    spread(0, xy, rxy)
 
     g_copy.wait_recv()
-    spread(4, g1, lambda d: rc.at[d, :, pl.ds(32, 16)])
-    rc[me, :, pl.ds(32, 16)] = g1[pl.ds(me * kept, kept)]
+    spread(1, g1, rcl)
 
     def pull_later(i):
         chain[i + 1, pl.ds(0, 16)] = dot_t(g1[i], wd[i]) + chain[links[0, i], pl.ds(0, 16)]
@@ -285,8 +313,7 @@
         e1[j] = jnp.concatenate([gate, push], 0).astype(BF16)
 
     each_block(blocks, gate_later)
-    spread(5, e1, lambda d: re.at[d, :, pl.ds(32, 16)])
-    re[me, :, pl.ds(32, 16)] = e1[pl.ds(me * kept, kept)]
+    spread(2, e1, rel)
 
     push_back(e1)
     settle(g1, in_rows(g_last))
@@ -303,22 +330,44 @@
     lower(h1, v1, in_rows(v_last))
     v_end = relay(3, v_last, v_out, after)
 
+    def products(side, k):
+        for half, (left, right) in enumerate(((rx, re), (ry, rc))):
+            yield half, dot_rows(left[side, :, k].reshape(row * 32, BLOCK), right[side, :, k].reshape(row * 32, BLOCK))
+
+    for side, copy in near:
+        if side == 1:
+            copy.wait_recv()
+    for k in range(kept):
+        for half, part in products(1, k):
+            crossing[half, k] = part.astype(BF16)
+    cross = pltpu.make_async_remote_copy(
+        src_ref=crossing,
+        dst_ref=crossed,
+        send_sem=link_send.at[4],
+        recv_sem=link_recv.at[4],
+        device_id={"dp": across},
+        device_id_type=MESH,
+    )
+    cross.start()
+    for side, copy in near:
+        if side == 0:
+            copy.wait_recv()
+    for k in range(kept):
+        for half, part in products(0, k):
+            total[half, k] = part
     for copy in sent:
         copy.wait_recv()
-
-    def rows_of(ref, k):
-        return ref[:, k].reshape(n_dp * 48, BLOCK)
-
+    cross.wait_recv()
     for k in range(kept):
-        for half, (left, right) in enumerate(((rx, re), (ry, rc))):
-            grad = lax.dot_general(
-                rows_of(left, k), rows_of(right, k), (((0,), (0,)), ((), ())), preferred_element_type=F32
-            )
+        for half, right in enumerate((rel, rcl)):
+            left = rxy[:, k, pl.ds(16 * half, 16)].reshape(n_dp * 16, BLOCK)
+            part = dot_rows(left, right[:, k].reshape(n_dp * 16, BLOCK))
+            grad = total[half, k] + crossed[half, k].astype(F32) + part
             grads[half, k] = (grad * scale).astype(BF16)
 
     grad_copy = pltpu.make_async_copy(grads, grads_out, in_sem.at[len(loads)])
     grad_copy.start()
-    for copy in sent:
+    for copy in sent + [copy for _, copy in near] + [cross]:
         copy.wait_send()
     grad_copy.wait()
     g_copy.wait_send()
@@ -391,24 +440,28 @@
             by_block(32, 2),
             by_block(8, 2),
             by_block(32),
-            by_block(48),
+            by_block(32),
             by_block(32),
             *[by_block(16)] * 5,
             *[pltpu.VMEM((2, 8, width), BF16)] * 2,
             pltpu.VMEM((2, kept, BLOCK, BLOCK), BF16),
-            by_block(48),
+            by_block(32),
             by_block(48),
             by_block(32),
             *[by_block(16)] * 3,
-            *[pltpu.VMEM((n_dp, kept, 48, BLOCK), BF16)] * 4,
+            by_block(32),
+            *[pltpu.VMEM((2, n_dp // 2, kept, 32, BLOCK), BF16)] * 4,
+            pltpu.VMEM((n_dp, kept, 32, BLOCK), BF16),
+            *[pltpu.VMEM((n_dp, kept, 16, BLOCK), BF16)] * 2,
+            *[pltpu.VMEM((2, kept, BLOCK, BLOCK), BF16)] * 2,
+            pltpu.VMEM((2, kept, BLOCK, BLOCK), F32),
             pltpu.VMEM((blocks + 1, 32, BLOCK), F32),
             pltpu.VMEM((blocks + 1, 16, BLOCK), F32),
             pltpu.VMEM((blocks, 32, BLOCK), F32),
             pltpu.SemaphoreType.DMA((17,)),
-            pltpu.SemaphoreType.DMA((6, n_dp - 1)),
-            pltpu.SemaphoreType.DMA((6, n_dp - 1)),
-            pltpu.SemaphoreType.DMA((4,)),
-            pltpu.SemaphoreType.DMA((4,)),
+            *[pltpu.SemaphoreType.DMA((4, 2, len(ALONG_X)))] * 2,
+            *[pltpu.SemaphoreType.DMA((3, n_dp - 1))] * 2,
+            *[pltpu.SemaphoreType.DMA((5,))] * 2,
         ],
         compiler_params=pltpu.CompilerParams(
             collective_id=0, has_side_effects=True, vmem_limit_bytes=56 << 20

time: 45 us -> 41.7 us (0.927)
  Pallas kernels: 42.3 us -> 39.3 us
    pallas_call x1, Pallas kernels: 40.4 us -> 37.4 us  [on_device(): pl.pallas_call(functools.partial(tick_kernel, n_section, n_dp, blocks, 1....]
where the time goes in v4:
time: 41.7 us; the launch traced here: 41.5 us
  Pallas kernels  39.3 us (94%)
  other arithmetic  0.9 us (2%)
  between operations  0.68 us (2%)
  local copies, waits for them, and re-layouts  0.65 us (2%)
    pallas_call x1, Pallas kernels, on_device(): pl.pallas_call(functools.partial(tick_kernel, n_section, n_dp, blocks, 1....  37.4 us
    pallas_call x1, Pallas kernels, on_device(): pl.pallas_call(hand_out, out_shape=(stream,) * 4 + (grad,) * 2, in_specs=...  1.86 us

profile of v4, /device:TPU:6, one launch (start us, length us, event | category | flops | bytes accessed | tf_op | source)
XLA Modules:
  0.0 41.5 jit_solution(15604659612270796990)
XLA Ops:
  0.7 0.0 copy-start
  0.7 0.0 copy-start.1
  0.7 0.6 %copy-done = s32[1,32]{1,0:T(1,128)S(1)} copy-done((s32[1,32]{1,0:T(1,128)S(1)}, s32[1,32]{1,0:T(1,128)}, u32[]{:S(2)}) %copy-start) | copy-done | bytes 152
  1.3 0.0 copy-done.1
  1.3 0.1 pad_add_fusion
  1.4 0.8 %select_reduce_fusion.links = s32[4,32]{1,0:T(4,128)} fusion(s32[32]{0:T(128)S(1)} %iota_add_fusion, s32[4,32]{1,0:T(4,128)S(1)} %get-tuple-element.14, s32[4,32]{1,0:T(4,128)S(1)} %get-tuple-element.13, s32[4,32]{1,0:T(4,128)S(1)} %get-tuple-element.12), kind=kLoop, calls=%fused_computation | loop fusion | flops 20352 | bytes 2176 | tf_op jit(solution)/shard_map/reduce_max | solution.py:409
  2.2 37.4 %ticks.1 = (bf16[2,8,4096]{2,1,0:T(8,128)(2,1)}, bf16[2,8,4096]{2,1,0:T(8,128)(2,1)}, bf16[2,4,128,128]{3,2,1,0:T(8,128)(2,1)}) custom-call(s32[1,32]{1,0:T(1,128)} %up_index.1, s32[1,32]{1,0:T(1,128)} %down_index.1, s32[1,2]{1,0:T(1,128)} %tick_order.1, s32[4,32]{1,0:T(4,128)} %select_reduce_fusion.links, bf16[1,32,128,128]{3,2,1,0:T(8,128)(2,1)} %w_up.1, ...), custom_call_target="tpu_custom_call" | custom-call | tf_op jit(solution)/shard_map/ticks/pallas_call | solution.py:425
  39.6 1.9 %hand_out.1 = (bf16[1,8,4096]{2,1,0:T(8,128)(2,1)}, bf16[1,8,4096]{2,1,0:T(8,128)(2,1)}, bf16[1,8,4096]{2,1,0:T(8,128)(2,1)}, bf16[1,8,4096]{2,1,0:T(8,128)(2,1)...) custom-call(bf16[2,8,4096]{2,1,0:T(8,128)(2,1)} %get-tuple-element.9.v, ...), custom_call_target="tpu_custom_call" | custom-call | tf_op jit(solution)/shard_map/hand_out/pallas_call | solution.py:473
  (3 shorter events, 0.0 us)
Async XLA Ops:
  0.7 0.7 %copy-start = (s32[1,32]{1,0:T(1,128)S(1)}, s32[1,32]{1,0:T(1,128)}, u32[]{:S(2)}) copy-start(s32[1,32]{1,0:T(1,128)} %up_index.1) | copy-start | bytes 388
  0.7 0.7 %copy-start.1 = (s32[1,32]{1,0:T(1,128)S(1)}, s32[1,32]{1,0:T(1,128)}, u32[]{:S(2)}) copy-start(s32[1,32]{1,0:T(1,128)} %down_index.1) | copy-start | bytes 388

commit v5 on v4

--- a/solution.py
+++ b/solution.py
@@ -58,14 +58,14 @@
 
 def tick_kernel(
     n_section, n_dp, blocks, scale,
-    up_index, down_index, tick_order, links,
+    up_index, down_index, tick_order, up_row, down_row,
     w_up, w_down, values_in, score_in, tangent_in, adjoint_in,
     saved_back, saved_tan, saved_second, saved_second_tan, saved_second_grad,
     v_out, g_out, grads_out,
     wu, wd, raw_x, raw_v, raw_c, x_slots, c_slots, xt, xs, cs,
     v0, v1, g1, v_sent, g_sent, v_last, g_last, grads,
     ys, yy, e0, e1, h0, h1, xy, rx, rc, ry, re, rxy, rcl, rel, crossing, crossed, total,
-    chain, chain2, keep,
+    chain, chain2, keep, links_row, links,
     in_sem, near_send, near_recv, send_sem, recv_sem, link_send, link_recv,
 ):
     section = lax.axis_index("section")
@@ -102,6 +102,17 @@
         pl.semaphore_signal(barrier, inc=1, device_id={"dp": lax.rem(me + p, n_dp)}, device_id_type=MESH)
     for s in (after, before):
         pl.semaphore_signal(barrier, inc=1, device_id={"section": s}, device_id_type=MESH)
+
+    rows = lax.broadcasted_iota(jnp.int32, (blocks, blocks), 0)
+    lanes = lax.broadcasted_iota(jnp.int32, (blocks, blocks), 1)
+    for at, index in enumerate((down_row, up_row)):
+        over = jnp.broadcast_to(index[...], (blocks, blocks))
+        down = jnp.max(jnp.where(rows == lanes, over, 0), axis=1, keepdims=True)
+        same = (down == over) & (rows < lanes)
+        links_row[pl.ds(at, 1)] = jnp.max(jnp.where(same, rows + 1, 0), axis=0, keepdims=True)
+        links_row[pl.ds(2 + at, 1)] = jnp.max(jnp.where(down == lanes, rows + 1, 0), axis=0, keepdims=True)
+    links_copy = pltpu.make_async_copy(links_row, links, in_sem.at[len(loads) + 1])
+    links_copy.start()
 
     first = tick_order[0, 0] * blocks
     later = tick_order[0, 1] * blocks
@@ -192,6 +203,7 @@
         xt[j, pl.ds(24, 8)] = x_slots[later + source, pl.ds(24, 8)]
 
     each_block(blocks, gather_v)
+    links_copy.wait()
     loads[early + 2].wait()
 
     def pull(i):
@@ -200,44 +212,38 @@
     each_block(blocks, pull)
     loads[early + 3].wait()
 
-    def raise_all(j):
-        z = dot(jnp.concatenate([xt[j], xs[j], xy[j, pl.ds(0, 16)]], 0), wu[j])
-        zv, zt, tan_f, tan_l = z[0:8], z[8:16], z[16:24], z[24:32]
-        back_f, za_f, ta_f = z[32:40], z[40:48], z[48:56]
-        ta_l, back_l, za_l = z[56:64], z[64:72], z[72:80]
+    def raise_first(j):
+        z = dot(jnp.concatenate([xt[j, pl.ds(0, 24)], xs[j, pl.ds(0, 24)]], 0), wu[j])
+        zv, zt, tan, back, za, ta = (z[8 * n : 8 * n + 8] for n in range(6))
         pulled = chain[links[2, j]]
-        pg, pa, ps_f, ps_l = pulled[0:8], pulled[8:16], pulled[16:24], pulled[24:32]
-        sig_f, sig_l = logistic(za_f), logistic(za_l)
-        slope_f, slope_l = slope_of(za_f, sig_f), slope_of(za_l, sig_l)
-        sig_bf, sig_bl = logistic(back_f), logistic(back_l)
+        pg, pa, ps = pulled[0:8], pulled[8:16], pulled[16:24]
+        sig, sig_back = logistic(za), logistic(back)
+        slope = slope_of(za, sig)
         hidden = silu_of(zv, logistic(zv))
-        tangent_hidden = slope_of(tan_f, logistic(tan_f)) * zt
+        tangent_hidden = slope_of(tan, logistic(tan)) * zt
         h0[j] = jnp.concatenate([hidden, tangent_hidden], 0).astype(BF16)
-        gate = slope_of(back_f, sig_bf) * pg
-        push = slope_f * pa + curve_of(za_f, sig_f) * ps_f * ta_f
-        e0[j] = jnp.concatenate([gate, push, slope_f * ps_f, slope_l * ps_l], 0).astype(BF16)
-        yy[j] = jnp.concatenate(
-            [
-                silu_of(back_f, sig_bf),
-                silu_of(za_f, sig_f),
-                slope_f * ta_f,
-                slope_l * ta_l,
-                silu_of(back_l, sig_bl),
-                silu_of(za_l, sig_l),
-            ],
-            0,
-        ).astype(BF16)
+        gate = slope_of(back, sig_back) * pg
+        push = slope * pa + curve_of(za, sig) * ps * ta
+        e0[j, pl.ds(0, 16)] = jnp.concatenate([gate, push], 0).astype(BF16)
+        e0[j, pl.ds(16, 8)] = (slope * ps).astype(BF16)
+        yy[j, pl.ds(0, 16)] = jnp.concatenate([silu_of(back, sig_back), silu_of(za, sig)], 0).astype(BF16)
+        yy[j, pl.ds(16, 8)] = (slope * ta).astype(BF16)
+
+    each_block(blocks, raise_first)
+
+    def raise_saved(j):
+        rows = jnp.concatenate([xt[j, pl.ds(24, 8)], xs[j, pl.ds(24, 8)], xy[j, pl.ds(0, 16)]], 0)
+        z = dot(rows, wu[j])
+        tan, ta, back, za = (z[8 * n : 8 * n + 8] for n in range(4))
+        ps = chain[links[2, j], pl.ds(24, 8)]
+        sig, sig_back = logistic(za), logistic(back)
+        slope = slope_of(za, sig)
+        e0[j, pl.ds(24, 8)] = (slope * ps).astype(BF16)
+        yy[j, pl.ds(24, 8)] = (slope * ta).astype(BF16)
+        yy[j, pl.ds(32, 16)] = jnp.concatenate([silu_of(back, sig_back), silu_of(za, sig)], 0).astype(BF16)
         keep[j] = jnp.concatenate(
-            [
-                slope_of(back_l, sig_bl),
-                slope_l,
-                curve_of(za_l, sig_l) * ps_l * ta_l,
-                slope_of(tan_l, logistic(tan_l)),
-            ],
-            0,
+            [slope_of(back, sig_back), slope, curve_of(za, sig) * ps * ta, slope_of(tan, logistic(tan))], 0
         )
-
-    each_block(blocks, raise_all)
 
     def push_back(source):
         def body(j):
@@ -287,6 +293,8 @@
     g_copy = relay(0, g_sent, g1, before)
     lower(h0, v0, in_block(v_sent))
     v_copy = relay(1, v_sent, v1, after)
+
+    each_block(blocks, raise_saved)
 
     def gather_y(i):
         source = down_index[0, i]
@@ -398,26 +406,15 @@
         copy.wait()
 
 
-def chain_links(down_index, up_index):
-    index = jnp.concatenate([down_index, up_index], 0)
-    count = index.shape[1]
-    spot = jnp.arange(count, dtype=jnp.int32)
-    own = jnp.concatenate([index, jnp.broadcast_to(spot, index.shape)], 0)
-    over = jnp.concatenate([index, index], 0)
-    limit = jnp.where(jnp.arange(4)[:, None] < 2, spot[None], count)
-    hit = (own[:, :, None] == over[:, None, :]) & (spot[None, None, :] < limit[:, :, None])
-    return jnp.max(jnp.where(hit, spot[None, None, :] + 1, 0), axis=2).astype(jnp.int32)
-
-
 def on_device(mesh_shape, *arrays):
     (w_up, up_index, w_down, down_index, tick_order, *rest) = arrays
     n_section, n_dp = mesh_shape["section"], mesh_shape["dp"]
     blocks = w_up.shape[1]
     rows, width = rest[0].shape[1:]
     kept = blocks // n_dp
-    links = chain_links(down_index, up_index)
     smem = pl.BlockSpec(memory_space=pltpu.SMEM)
     hbm = pl.BlockSpec(memory_space=pltpu.HBM)
+    vmem = pl.BlockSpec(memory_space=pltpu.VMEM)
 
     def by_block(height, copies=1):
         return pltpu.VMEM((copies * blocks, height, BLOCK), BF16)
@@ -429,7 +426,7 @@
             jax.ShapeDtypeStruct((2, rows, width), BF16),
             jax.ShapeDtypeStruct((2, kept, BLOCK, BLOCK), BF16),
         ),
-        in_specs=[smem] * 4 + [hbm] * 11,
+        in_specs=[smem] * 3 + [vmem] * 2 + [hbm] * 11,
         out_specs=(hbm, hbm, hbm),
         scratch_shapes=[
             pltpu.VMEM((blocks, BLOCK, BLOCK), BF16),
@@ -458,7 +455,9 @@
             pltpu.VMEM((blocks + 1, 32, BLOCK), F32),
             pltpu.VMEM((blocks + 1, 16, BLOCK), F32),
             pltpu.VMEM((blocks, 32, BLOCK), F32),
-            pltpu.SemaphoreType.DMA((17,)),
+            pltpu.VMEM((4, blocks), jnp.int32),
+            pltpu.SMEM((4, blocks), jnp.int32),
+            pltpu.SemaphoreType.DMA((18,)),
             *[pltpu.SemaphoreType.DMA((4, 2, len(ALONG_X)))] * 2,
             *[pltpu.SemaphoreType.DMA((3, n_dp - 1))] * 2,
             *[pltpu.SemaphoreType.DMA((5,))] * 2,
@@ -467,7 +466,7 @@
             collective_id=0, has_side_effects=True, vmem_limit_bytes=56 << 20
         ),
         name="ticks",
-    )(up_index, down_index, tick_order, links, w_up, w_down, *rest)
+    )(up_index, down_index, tick_order, up_index, down_index, w_up, w_down, *rest)
     stream = jax.ShapeDtypeStruct((1, rows, width), BF16)
     grad = jax.ShapeDtypeStruct((1, kept, BLOCK, BLOCK), BF16)
     return pl.pallas_call(

time: 41.7 us -> 40.2 us (0.964)
  other arithmetic: 0.9 us -> 0 us
  local copies, waits for them, and re-layouts: 0.65 us -> 0 us
    reduce_max x1 -> x0, other arithmetic: 0.82 us -> none  [chain_links(): jnp.max(jnp.where(hit, spot[None, None, :] + 1, 0), axis=2)]
    unnamed x4 -> x0, local copies, waits for them, and re-layouts: 0.65 us -> none
where the time goes in v5:
time: 40.2 us; the launch traced here: 40 us
  Pallas kernels  39.4 us (98%)
  between operations  0.65 us (2%)
    pallas_call x1, Pallas kernels, on_device(): pl.pallas_call(functools.partial(tick_kernel, n_section, n_dp, blocks, 1....  37.5 us
    pallas_call x1, Pallas kernels, on_device(): pl.pallas_call(hand_out, out_shape=(stream,) * 4 + (grad,) * 2, in_specs=...  1.86 us

profile of v5, /device:TPU:6, one launch (start us, length us, event | category | flops | bytes accessed | tf_op | source)
XLA Modules:
  0.0 40.0 jit_solution(833211652188498120)
XLA Ops:
  0.6 37.5 %ticks.1 = (bf16[2,8,4096]{2,1,0:T(8,128)(2,1)}, bf16[2,8,4096]{2,1,0:T(8,128)(2,1)}, bf16[2,4,128,128]{3,2,1,0:T(8,128)(2,1)}) custom-call(s32[1,32]{1,0:T(1,128)} %up_row.1, s32[1,32]{1,0:T(1,128)} %down_row.1, s32[1,2]{1,0:T(1,128)} %tick_order.1, s32[1,32]{1,0:T(1,128)} %up_row.1, s32[1,32]{1,0:T(1,128)} %down_row.1, bf16[1,32,128,128]{3,2,1,0:T(8,128)(2,1)} %w_up.1, ...), custom_call_target="tpu_custom_call" | custom-call | tf_op jit(solution)/shard_map/ticks/pallas_call | solution.py:422
  38.1 1.9 %hand_out.1 = (bf16[1,8,4096]{2,1,0:T(8,128)(2,1)}, bf16[1,8,4096]{2,1,0:T(8,128)(2,1)}, bf16[1,8,4096]{2,1,0:T(8,128)(2,1)}, bf16[1,8,4096]{2,1,0:T(8,128)(2,1)...) custom-call(bf16[2,8,4096]{2,1,0:T(8,128)(2,1)} %get-tuple-element.9.v, ...), custom_call_target="tpu_custom_call" | custom-call | tf_op jit(solution)/shard_map/hand_out/pallas_call | solution.py:472

commit v6 on v5

--- a/solution.py
+++ b/solution.py
@@ -63,7 +63,7 @@
     saved_back, saved_tan, saved_second, saved_second_tan, saved_second_grad,
     v_out, g_out, grads_out,
     wu, wd, raw_x, raw_v, raw_c, x_slots, c_slots, xt, xs, cs,
-    v0, v1, g1, v_sent, g_sent, v_last, g_last, grads,
+    v0, v1, g1, v_sent, g_sent, v_last, g_last,
     ys, yy, e0, e1, h0, h1, xy, rx, rc, ry, re, rxy, rcl, rel, crossing, crossed, total,
     chain, chain2, keep, links_row, links,
     in_sem, near_send, near_recv, send_sem, recv_sem, link_send, link_recv,
@@ -77,6 +77,12 @@
     my_x, my_y = me % row, me // row
     across = (1 - my_y) * row + my_x
 
+    barrier = pltpu.get_barrier_semaphore()
+    for p in range(1, n_dp):
+        pl.semaphore_signal(barrier, inc=1, device_id={"dp": lax.rem(me + p, n_dp)}, device_id_type=MESH)
+    for s in (after, before):
+        pl.semaphore_signal(barrier, inc=1, device_id={"section": s}, device_id_type=MESH)
+
     loads = []
 
     def load(source, target):
@@ -97,12 +103,6 @@
     load(w_down.at[0], wd)
     load(w_up.at[0], wu)
 
-    barrier = pltpu.get_barrier_semaphore()
-    for p in range(1, n_dp):
-        pl.semaphore_signal(barrier, inc=1, device_id={"dp": lax.rem(me + p, n_dp)}, device_id_type=MESH)
-    for s in (after, before):
-        pl.semaphore_signal(barrier, inc=1, device_id={"section": s}, device_id_type=MESH)
-
     rows = lax.broadcasted_iota(jnp.int32, (blocks, blocks), 0)
     lanes = lax.broadcasted_iota(jnp.int32, (blocks, blocks), 1)
     for at, index in enumerate((down_row, up_row)):
@@ -111,7 +111,7 @@
         same = (down == over) & (rows < lanes)
         links_row[pl.ds(at, 1)] = jnp.max(jnp.where(same, rows + 1, 0), axis=0, keepdims=True)
         links_row[pl.ds(2 + at, 1)] = jnp.max(jnp.where(down == lanes, rows + 1, 0), axis=0, keepdims=True)
-    links_copy = pltpu.make_async_copy(links_row, links, in_sem.at[len(loads) + 1])
+    links_copy = pltpu.make_async_copy(links_row, links, in_sem.at[len(loads)])
     links_copy.start()
 
     first = tick_order[0, 0] * blocks
@@ -371,38 +371,25 @@
             left = rxy[:, k, pl.ds(16 * half, 16)].reshape(n_dp * 16, BLOCK)
             part = dot_rows(left, right[:, k].reshape(n_dp * 16, BLOCK))
             grad = total[half, k] + crossed[half, k].astype(F32) + part
-            grads[half, k] = (grad * scale).astype(BF16)
-
-    grad_copy = pltpu.make_async_copy(grads, grads_out, in_sem.at[len(loads)])
-    grad_copy.start()
+            grads_out[half, k] = (grad * scale).astype(BF16)
+
     for copy in sent + [copy for _, copy in near] + [cross]:
         copy.wait_send()
-    grad_copy.wait()
     g_copy.wait_send()
     v_copy.wait_send()
     g_end.wait()
     v_end.wait()
 
 
-def hand_out(v, g, grads, values, score, tangent, adjoint, up, down, held, held_grads, in_sem, out_sem):
-    moves = (
-        (v, 0, values, held.at[0]),
-        (v, 1, tangent, held.at[1]),
-        (g, 0, score, held.at[2]),
-        (g, 1, adjoint, held.at[3]),
-        (grads, 0, up, held_grads.at[0]),
-        (grads, 1, down, held_grads.at[1]),
-    )
-    inward = [
-        pltpu.make_async_copy(source.at[half], stop, in_sem.at[n]) for n, (source, half, _, stop) in enumerate(moves)
+def hand_out(v, g, grads, values, score, tangent, adjoint, up, down, sem):
+    moves = ((v, 0, values), (v, 1, tangent), (g, 0, score), (g, 1, adjoint), (grads, 0, up), (grads, 1, down))
+    copies = [
+        pltpu.make_async_copy(source.at[half], target.at[0], sem.at[n])
+        for n, (source, half, target) in enumerate(moves)
     ]
-    outward = [pltpu.make_async_copy(stop, target.at[0], out_sem.at[n]) for n, (_, _, target, stop) in enumerate(moves)]
-    for copy in inward:
+    for copy in copies:
         copy.start()
-    for arrived, copy in zip(inward, outward):
-        arrived.wait()
-        copy.start()
-    for copy in outward:
+    for copy in copies:
         copy.wait()
 
 
@@ -422,12 +409,12 @@
     v, g, grads = pl.pallas_call(
         functools.partial(tick_kernel, n_section, n_dp, blocks, 1.0 / (rows * n_dp)),
         out_shape=(
-            jax.ShapeDtypeStruct((2, rows, width), BF16),
-            jax.ShapeDtypeStruct((2, rows, width), BF16),
-            jax.ShapeDtypeStruct((2, kept, BLOCK, BLOCK), BF16),
+            pltpu.VMEM((2, rows, width), BF16),
+            pltpu.VMEM((2, rows, width), BF16),
+            pltpu.VMEM((2, kept, BLOCK, BLOCK), BF16),
         ),
         in_specs=[smem] * 3 + [vmem] * 2 + [hbm] * 11,
-        out_specs=(hbm, hbm, hbm),
+        out_specs=(vmem, vmem, vmem),
         scratch_shapes=[
             pltpu.VMEM((blocks, BLOCK, BLOCK), BF16),
             pltpu.VMEM((blocks, BLOCK, BLOCK), BF16),
@@ -441,7 +428,6 @@
             by_block(32),
             *[by_block(16)] * 5,
             *[pltpu.VMEM((2, 8, width), BF16)] * 2,
-            pltpu.VMEM((2, kept, BLOCK, BLOCK), BF16),
             by_block(32),
             by_block(48),
             by_block(32),
@@ -457,7 +443,7 @@
             pltpu.VMEM((blocks, 32, BLOCK), F32),
             pltpu.VMEM((4, blocks), jnp.int32),
             pltpu.SMEM((4, blocks), jnp.int32),
-            pltpu.SemaphoreType.DMA((18,)),
+            pltpu.SemaphoreType.DMA((17,)),
             *[pltpu.SemaphoreType.DMA((4, 2, len(ALONG_X)))] * 2,
             *[pltpu.SemaphoreType.DMA((3, n_dp - 1))] * 2,
             *[pltpu.SemaphoreType.DMA((5,))] * 2,
@@ -472,15 +458,10 @@
     return pl.pallas_call(
         hand_out,
         out_shape=(stream,) * 4 + (grad,) * 2,
-        in_specs=[hbm] * 3,
+        in_specs=[vmem] * 3,
         out_specs=(hbm,) * 6,
-        scratch_shapes=[
-            pltpu.VMEM((4, rows, width), BF16),
-            pltpu.VMEM((2, kept, BLOCK, BLOCK), BF16),
-            pltpu.SemaphoreType.DMA((6,)),
-            pltpu.SemaphoreType.DMA((6,)),
-        ],
-        compiler_params=pltpu.CompilerParams(vmem_limit_bytes=56 << 20),
+        scratch_shapes=[pltpu.SemaphoreType.DMA((6,))],
+        compiler_params=pltpu.CompilerParams(vmem_limit_bytes=8 << 20),
         name="hand_out",
     )(v, g, grads)
 

time: 40.2 us -> 38.5 us (0.958)
  Pallas kernels: 39.4 us -> 37.7 us
    pallas_call x1, Pallas kernels: 1.86 us -> 0.84 us  [on_device(): pl.pallas_call(hand_out, out_shape=(stream,) * 4 + (grad,) * 2, in_specs=...]
    pallas_call x1, Pallas kernels: 37.5 us -> 36.9 us  [on_device(): pl.pallas_call(functools.partial(tick_kernel, n_section, n_dp, blocks, 1....]
where the time goes in v6:
time: 38.5 us; the launch traced here: 38.3 us
  Pallas kernels  37.7 us (98%)
  between operations  0.65 us (2%)
    pallas_call x1, Pallas kernels, on_device(): pl.pallas_call(functools.partial(tick_kernel, n_section, n_dp, blocks, 1....  36.9 us
    pallas_call x1, Pallas kernels, on_device(): pl.pallas_call(hand_out, out_shape=(stream,) * 4 + (grad,) * 2, in_specs=...  0.84 us

profile of v6, /device:TPU:6, one launch (start us, length us, event | category | flops | bytes accessed | tf_op | source)
XLA Modules:
  0.0 38.3 jit_solution(551899900302089663)
XLA Ops:
  0.6 36.9 %ticks.1 = (bf16[2,8,4096]{2,1,0:T(8,128)(2,1)S(1)}, bf16[2,8,4096]{2,1,0:T(8,128)(2,1)S(1)}, bf16[2,4,128,128]{3,2,1,0:T(8,128)(2,1)S(1)}) custom-call(s32[1,32]{1,0:T(1,128)} %up_row.1, s32[1,32]{1,0:T(1,128)} %down_row.1, s32[1,2]{1,0:T(1,128)} %tick_order.1, s32[1,32]{1,0:T(1,128)} %up_row.1, s32[1,32]{1,0:T(1,128)} %down_row.1, ...), custom_call_target="tpu_custom_call" | custom-call | tf_op jit(solution)/shard_map/ticks/pallas_call | solution.py:409
  37.5 0.8 %hand_out.1 = (bf16[1,8,4096]{2,1,0:T(8,128)(2,1)}, bf16[1,8,4096]{2,1,0:T(8,128)(2,1)}, bf16[1,8,4096]{2,1,0:T(8,128)(2,1)}, bf16[1,8,4096]{2,1,0:T(8,128)(2,1)...) custom-call(bf16[2,8,4096]{2,1,0:T(8,128)(2,1)S(1)} %get-tuple-element.9.v, ...), custom_call_target="tpu_custom_call" | custom-call | tf_op jit(solution)/shard_map/hand_out/pallas_call | solution.py:458

commit v7 on v6

--- a/solution.py
+++ b/solution.py
@@ -64,7 +64,7 @@
     v_out, g_out, grads_out,
     wu, wd, raw_x, raw_v, raw_c, x_slots, c_slots, xt, xs, cs,
     v0, v1, g1, v_sent, g_sent, v_last, g_last,
-    ys, yy, e0, e1, h0, h1, xy, rx, rc, ry, re, rxy, rcl, rel, crossing, crossed, total,
+    ys, yy, e0, e1, h0, h1, xl, yl, rx, rc, ry, re, rxl, ryl, rcl, rel, crossing, crossed, total,
     chain, chain2, keep, links_row, links,
     in_sem, near_send, near_recv, send_sem, recv_sem, link_send, link_recv,
 ):
@@ -136,7 +136,7 @@
         source = up_index[0, j]
         xs[j, pl.ds(0, 24)] = x_slots[first + source, pl.ds(0, 24)]
         xs[j, pl.ds(24, 8)] = x_slots[later + source, pl.ds(16, 8)]
-        xy[j, pl.ds(0, 16)] = x_slots[later + source, pl.ds(0, 16)]
+        xl[j] = x_slots[later + source, pl.ds(0, 16)]
         cs[j, pl.ds(16, 8)] = c_slots[first + j]
         cs[j, pl.ds(24, 8)] = c_slots[later + j]
 
@@ -186,6 +186,7 @@
             sent.append(copy)
         landing[me] = source[pl.ds(me * kept, kept)]
 
+    spread(0, xl, rxl)
     spread_near((0, xs, rx), (1, cs, rc))
 
     for copy in loads[early : early + 2]:
@@ -232,7 +233,7 @@
     each_block(blocks, raise_first)
 
     def raise_saved(j):
-        rows = jnp.concatenate([xt[j, pl.ds(24, 8)], xs[j, pl.ds(24, 8)], xy[j, pl.ds(0, 16)]], 0)
+        rows = jnp.concatenate([xt[j, pl.ds(24, 8)], xs[j, pl.ds(24, 8)], xl[j]], 0)
         z = dot(rows, wu[j])
         tan, ta, back, za = (z[8 * n : 8 * n + 8] for n in range(4))
         ps = chain[links[2, j], pl.ds(24, 8)]
@@ -299,14 +300,13 @@
     def gather_y(i):
         source = down_index[0, i]
         ys[i] = yy[source, pl.ds(0, 32)]
-        xy[i, pl.ds(16, 16)] = yy[source, pl.ds(32, 16)]
+        yl[i] = yy[source, pl.ds(32, 16)]
 
     each_block(blocks, gather_y)
     spread_near((2, ys, ry), (3, e0, re))
-    spread(0, xy, rxy)
+    spread(3, yl, ryl)
 
     g_copy.wait_recv()
-    spread(1, g1, rcl)
 
     def pull_later(i):
         chain[i + 1, pl.ds(0, 16)] = dot_t(g1[i], wd[i]) + chain[links[0, i], pl.ds(0, 16)]
@@ -321,11 +321,12 @@
         e1[j] = jnp.concatenate([gate, push], 0).astype(BF16)
 
     each_block(blocks, gate_later)
-    spread(2, e1, rel)
 
     push_back(e1)
     settle(g1, in_rows(g_last))
     g_end = relay(2, g_last, g_out, before)
+    spread(1, g1, rcl)
+    spread(2, e1, rel)
 
     v_copy.wait_recv()
 
@@ -367,9 +368,8 @@
         copy.wait_recv()
     cross.wait_recv()
     for k in range(kept):
-        for half, right in enumerate((rel, rcl)):
-            left = rxy[:, k, pl.ds(16 * half, 16)].reshape(n_dp * 16, BLOCK)
-            part = dot_rows(left, right[:, k].reshape(n_dp * 16, BLOCK))
+        for half, (left, right) in enumerate(((rxl, rel), (ryl, rcl))):
+            part = dot_rows(left[:, k].reshape(n_dp * 16, BLOCK), right[:, k].reshape(n_dp * 16, BLOCK))
             grad = total[half, k] + crossed[half, k].astype(F32) + part
             grads_out[half, k] = (grad * scale).astype(BF16)
 
@@ -431,11 +431,9 @@
             by_block(32),
             by_block(48),
             by_block(32),
-            *[by_block(16)] * 3,
-            by_block(32),
+            *[by_block(16)] * 5,
             *[pltpu.VMEM((2, n_dp // 2, kept, 32, BLOCK), BF16)] * 4,
-            pltpu.VMEM((n_dp, kept, 32, BLOCK), BF16),
-            *[pltpu.VMEM((n_dp, kept, 16, BLOCK), BF16)] * 2,
+            *[pltpu.VMEM((n_dp, kept, 16, BLOCK), BF16)] * 4,
             *[pltpu.VMEM((2, kept, BLOCK, BLOCK), BF16)] * 2,
             pltpu.VMEM((2, kept, BLOCK, BLOCK), F32),
             pltpu.VMEM((blocks + 1, 32, BLOCK), F32),
@@ -445,7 +443,7 @@
             pltpu.SMEM((4, blocks), jnp.int32),
             pltpu.SemaphoreType.DMA((17,)),
             *[pltpu.SemaphoreType.DMA((4, 2, len(ALONG_X)))] * 2,
-            *[pltpu.SemaphoreType.DMA((3, n_dp - 1))] * 2,
+            *[pltpu.SemaphoreType.DMA((4, n_dp - 1))] * 2,
             *[pltpu.SemaphoreType.DMA((5,))] * 2,
         ],
         compiler_params=pltpu.CompilerParams(

time: 38.5 us -> 38.4 us (level)
  no operation moved by 1% of the time
where the time goes in v7:
time: 38.4 us; the launch traced here: 38.2 us
  Pallas kernels  37.5 us (98%)
  between operations  0.65 us (2%)
    pallas_call x1, Pallas kernels, on_device(): pl.pallas_call(functools.partial(tick_kernel, n_section, n_dp, blocks, 1....  36.7 us
    pallas_call x1, Pallas kernels, on_device(): pl.pallas_call(hand_out, out_shape=(stream,) * 4 + (grad,) * 2, in_specs=...  0.84 us

profile of v7, /device:TPU:6, one launch (start us, length us, event | category | flops | bytes accessed | tf_op | source)
XLA Modules:
  0.0 38.2 jit_solution(8001883676203365356)
XLA Ops:
  0.6 36.7 %ticks.1 = (bf16[2,8,4096]{2,1,0:T(8,128)(2,1)S(1)}, bf16[2,8,4096]{2,1,0:T(8,128)(2,1)S(1)}, bf16[2,4,128,128]{3,2,1,0:T(8,128)(2,1)S(1)}) custom-call(s32[1,32]{1,0:T(1,128)} %up_row.1, s32[1,32]{1,0:T(1,128)} %down_row.1, s32[1,2]{1,0:T(1,128)} %tick_order.1, s32[1,32]{1,0:T(1,128)} %up_row.1, s32[1,32]{1,0:T(1,128)} %down_row.1, ...), custom_call_target="tpu_custom_call" | custom-call | tf_op jit(solution)/shard_map/ticks/pallas_call | solution.py:409
  37.4 0.8 %hand_out.1 = (bf16[1,8,4096]{2,1,0:T(8,128)(2,1)}, bf16[1,8,4096]{2,1,0:T(8,128)(2,1)}, bf16[1,8,4096]{2,1,0:T(8,128)(2,1)}, bf16[1,8,4096]{2,1,0:T(8,128)(2,1)...) custom-call(bf16[2,8,4096]{2,1,0:T(8,128)(2,1)S(1)} %get-tuple-element.9.v, ...), custom_call_target="tpu_custom_call" | custom-call | tf_op jit(solution)/shard_map/hand_out/pallas_call | solution.py:456
